TPU v7x, 256 devices: a whole 4x4x8 slice. The times are simulated.
256 devices in a mesh: patch: 64 (over z, y, core), mp: 4 (over x).
Axes of the slice: x: 4, y: 4, z: 8, core: 2. Of those that a mesh axis runs over, the one named last changes fastest.
Arguments:
- grid_latent: bfloat16 [65536, 512], P('patch'), may hold values from -6 to 6
- mesh_latent: bfloat16 [8192, 512], P('patch', 'mp'), may hold values from -6 to 6
- edge_weight: bfloat16 [768, 128, 128], P('patch'), may hold values from -0.15625 to 0.15625
- block_source: int32 [768], P('patch'), may hold values from 0 to 511, as said below
- block_live: int32 [768], P('patch'), may hold values from 0 to 1
- mlp_first: bfloat16 [512, 512], replicated, may hold values from -0.25 to 0.25
- mlp_second: bfloat16 [512, 512], P(None, 'mp'), may hold values from -0.25 to 0.25
- mesh_cotangent: bfloat16 [8192, 512], P('patch', 'mp'), may hold values from -6 to 6
Outputs:
- mesh_out: bfloat16 [8192, 512], P('patch', 'mp')
- grad_first: float32 [512, 512], P(None, 'mp')
- grad_second: float32 [512, 512], P(None, 'mp')
Inputs may be any that keep to these rules, and one draw needn't show every extreme that they name: `block_source`: grid patch g lies on the device of index g // 8 along patch, and slot b on the device of index b // 12. On every device at most 1 slots take their source from one device, and some device supplies exactly 1 slots to some device.
All inputs are finite; a program needn't handle non-finite values.
Results may differ from a plain program's by a relative error of at most 0.0058.
Values may be sent and summed in bfloat16 or wider, within the bound.
A program may use at most 64 MiB of HBM per device.

v0:
```python
import functools
import math

import jax
import jax.numpy as jnp
from jax import lax
from jax.sharding import Mesh
from jax.sharding import PartitionSpec as P

PATCH = 128
GPD = 8
BPM = 12
MPD = 1
EBD = 12
PATCH_AXES = ("patch_0", "patch_1", "patch_2")


def joined_along(parts, dim):
    parts = jnp.moveaxis(parts, 0, dim)
    lengths = parts.shape
    return parts.reshape(*lengths[:dim], lengths[dim] * lengths[dim + 1], *lengths[dim + 2 :])


def one_gather(arrays, axis, dims):
    flat = jnp.concatenate([a.reshape(-1) for a in arrays])
    lines, at, finished = (lax.all_gather(flat, axis), 0, [])
    for a, dim in zip(arrays, dims):
        parts = lines[:, at : at + a.size].reshape(-1, *a.shape)
        finished.append(joined_along(parts, dim))
        at += a.size
    return tuple(finished)


def one_axis_at_a_time(array, axes):
    return functools.reduce(lax.psum, axes, array)


def silu_slope(values):
    sigmoid = jax.nn.sigmoid(values)
    return sigmoid * (1.0 + values * (1.0 - sigmoid))


def per_device(
    grid_latent,
    mesh_latent,
    edge_weight,
    block_source,
    block_live,
    mlp_first,
    mlp_second,
    mesh_cotangent,
):
    devices = lax.axis_size(PATCH_AXES)
    own_index = lax.axis_index(PATCH_AXES)
    column_index = lax.axis_index("mp")
    grid_rows = grid_latent.shape[0]
    width_local = mlp_second.shape[1]
    hidden_local = mlp_first.shape[1] // lax.axis_size("mp")
    block_width = PATCH * width_local
    slot_cap = (EBD + devices - 1) // devices
    pre_act = jnp.dot(grid_latent, mlp_first, preferred_element_type=jnp.float32)
    hidden = jax.nn.silu(pre_act).astype(jnp.bfloat16)
    message = jnp.dot(hidden, mlp_second, preferred_element_type=jnp.float32).astype(jnp.bfloat16)
    message_flat = message.reshape(GPD, block_width)
    live_local = block_live.astype(jnp.float32)[:, None, None]
    every_source, every_live = one_gather((block_source, block_live), PATCH_AXES, (0, 0))
    every_source = every_source.reshape(devices, EBD)
    every_live = every_live.reshape(devices, EBD)
    source_device = every_source // GPD
    source_patch = every_source % GPD
    slot_order = jnp.arange(EBD)
    same_source = (source_device[:, :, None] == source_device[:, None, :]) & (
        slot_order[None, None, :] < slot_order[None, :, None]
    )
    slot_rank = jnp.sum(same_source, axis=2)
    own_sources = source_device[own_index]
    own_ranks = slot_rank[own_index]
    wanted = (source_device == own_index) & (every_live == 1)
    matches = (
        wanted[:, :, None, None]
        & (slot_rank[:, :, None, None] == jnp.arange(slot_cap)[None, None, :, None])
        & (source_patch[:, :, None, None] == jnp.arange(GPD)[None, None, None, :])
    )
    picking = jnp.sum(matches, axis=1).reshape(devices * slot_cap, GPD).astype(jnp.bfloat16)
    outgoing = (
        jnp.dot(picking, message_flat, preferred_element_type=jnp.float32)
        .astype(jnp.bfloat16)
        .reshape(devices, slot_cap, block_width)
    )
    incoming = lax.all_to_all(
        outgoing, PATCH_AXES, split_axis=0, concat_axis=0, tiled=True
    ).reshape(devices * slot_cap, block_width)
    lookup = own_sources * slot_cap + own_ranks
    block_input = jnp.take(incoming, lookup, axis=0).reshape(EBD, PATCH, width_local)
    products = (
        jnp.einsum("bpq,bqc->bpc", edge_weight, block_input, preferred_element_type=jnp.float32)
        * live_local
    )
    summed = (
        products.reshape(MPD, BPM, PATCH, width_local).sum(axis=1).reshape(MPD * PATCH, width_local)
    )
    mesh_out = (mesh_latent.astype(jnp.float32) + summed).astype(jnp.bfloat16)
    cotangent_blocks = jnp.broadcast_to(
        mesh_cotangent.reshape(MPD, 1, PATCH, width_local), (MPD, BPM, PATCH, width_local)
    ).reshape(EBD, PATCH, width_local)
    adjoint = (
        jnp.einsum(
            "bqp,bqc->bpc", edge_weight, cotangent_blocks, preferred_element_type=jnp.float32
        )
        * live_local
    ).astype(jnp.bfloat16)
    adjoint = adjoint.reshape(EBD, block_width)
    slot_rows = devices * slot_cap
    scatter_table = (
        (jnp.arange(slot_rows)[:, None] == lookup[None, :]) & (block_live[None, :] == 1)
    ).astype(jnp.bfloat16)
    returning = jnp.dot(scatter_table, adjoint, preferred_element_type=jnp.float32).astype(
        jnp.bfloat16
    )
    back_flat = lax.all_to_all(
        returning.reshape(devices, slot_cap, block_width),
        PATCH_AXES,
        split_axis=0,
        concat_axis=0,
        tiled=True,
    ).reshape(devices * slot_cap, block_width)
    grad_message = lax.dot_general(
        picking, back_flat, (((0,), (0,)), ((), ())), preferred_element_type=jnp.float32
    )
    grad_message = grad_message.astype(jnp.bfloat16).reshape(grid_rows, width_local)
    scaling = 1.0 / math.sqrt(grid_rows * devices)
    grad_second = (
        lax.dot_general(
            hidden, grad_message, (((0,), (0,)), ((), ())), preferred_element_type=jnp.float32
        )
        * scaling
    )
    grad_piece = lax.all_gather(grad_message, "mp", axis=1, tiled=True)
    second_piece = lax.all_gather(mlp_second, "mp", axis=1, tiled=True)
    rows_of_second = lax.dynamic_slice_in_dim(
        second_piece, column_index * hidden_local, hidden_local, 0
    )
    grad_hidden = lax.dot_general(
        rows_of_second, grad_piece, (((1,), (1,)), ((), ())), preferred_element_type=jnp.float32
    )
    pre_slice = lax.dynamic_slice_in_dim(pre_act, column_index * hidden_local, hidden_local, 1).T
    grad_pre = (grad_hidden * silu_slope(pre_slice)).astype(jnp.bfloat16)
    grad_first = (
        lax.dot_general(
            grid_latent, grad_pre, (((0,), (1,)), ((), ())), preferred_element_type=jnp.float32
        )
        * scaling
    )
    grad_first, grad_second = (
        one_axis_at_a_time(grad_first, PATCH_AXES),
        one_axis_at_a_time(grad_second, PATCH_AXES),
    )
    return (mesh_out, grad_first, grad_second)


def solution(mesh):
    torus = Mesh(
        mesh.devices.reshape(8, 4, 2, mesh.shape["mp"]), ("patch_0", "patch_1", "patch_2", "mp")
    )
    in_specs = (
        P(PATCH_AXES, None),
        P(PATCH_AXES, "mp"),
        P(PATCH_AXES, None, None),
        P(PATCH_AXES),
        P(PATCH_AXES),
        P(),
        P(None, "mp"),
        P(PATCH_AXES, "mp"),
    )
    out_specs = (P(PATCH_AXES, "mp"), P(None, "mp"), P(None, "mp"))
    return jax.shard_map(
        per_device, mesh=torus, in_specs=in_specs, out_specs=out_specs, check_vma=False
    )
```

profile of v0, /device:TPU:1, one launch (start us, length us, event | category | flops | bytes accessed | tf_op | source)
XLA Modules:
  0.0 328.0 jit_solution(325961317000444766)
XLA Ops:
  11.4 21.0 %all-reduce = s32[1536]{0:T(1024)S(1)} all-reduce(s32[1536]{0:T(1024)S(1)} %add_dynamic-update-slice_fusion), channel_id=2, replica_groups=mesh['patch_0'=8,'patch_1'=4,'patch_2'=2,'mp'=4] {'patch_0','patch_1','p..., use_global_device_ids=true, to_apply=%add | all-reduce | flops 1536 | bytes 12288
  36.1 1.7 fusion.1
  38.4 2.9 reduce.8
  41.2 4.5 %reshape.158 = bf16[64,2,8192]{2,1,0:T(2,128)(2,1)} reshape(bf16[64,16384]{1,0:T(8,128)(2,1)} %reduce.8) | data formatting | bytes 4194304
  45.7 8.9 %all-to-all-start.1 = ((bf16[64,2,8192]{2,1,0:T(2,128)(2,1)}), bf16[64,2,8192]{2,1,0:T(2,128)(2,1)S(1)}, u32[]{:S(2)}, u32[]{:S(2)}) async-start(bf16[64,2,8192]{2,1,0:T(2,128)(2,1)} %reshape.158), calls=%async_computation.1 | async-start | bytes 4194304 | tf_op jit(solution)/shard_map/all_to_all | solution.py:120
  55.3 3.3 %multiply_convert_fusion = (bf16[1024,512]{1,0:T(8,128)(2,1)S(1)}, f32[1024,512]{1,0:T(8,128)}) fusion(bf16[1024,512]{1,0:T(8,128)(2,1)S(1)} %copy-done, bf16[512,512]{1,0:T(8,128)(2,1)} %param.13), kind=kOutput, calls=%fused_computation.9 | convolution fusion | flops 539492352 | bytes 4718592 | tf_op jit(solution)/shard_map/dot_general | solution.py:61
  63.2 2.1 fusion
  65.3 4.5 %reduce.7 = bf16[64,16384]{1,0:T(8,128)(2,1)} reduce(bf16[64,1,16384]{2,0,1:T(8,128)(2,1)} %fusion, bf16[]{:T(256)} %broadcast.136), dimensions={1}, to_apply=%copy.46.reduce_sub_computation | reduce | bytes 4194306 | tf_op jit(solution)/shard_map/reshape | solution.py:88
  69.8 4.5 %reshape.156 = bf16[64,2,8192]{2,1,0:T(2,128)(2,1)} reshape(bf16[64,16384]{1,0:T(8,128)(2,1)} %reduce.7) | data formatting | bytes 4194304
  74.3 30.3 %all-to-all-done.1 = bf16[64,2,8192]{2,1,0:T(2,128)(2,1)S(1)} async-done(((bf16[64,2,8192]{2,1,0:T(2,128)(2,1)}), bf16[64,2,8192]{2,1,0:T(2,128)(2,1)S(1)}, u32[]{:S(2)}, u32[]{:S(2)}) %all-to-all-start.1) | async-done | bytes 2097184 | tf_op jit(solution)/shard_map/all_to_all | solution.py:120
  106.0 6.8 %all-to-all-start = ((bf16[64,2,8192]{2,1,0:T(2,128)(2,1)}), bf16[64,2,8192]{2,1,0:T(2,128)(2,1)S(1)}, u32[]{:S(2)}, u32[]{:S(2)}) async-start(bf16[64,2,8192]{2,1,0:T(2,128)(2,1)} %reshape.156), calls=%async_computation | async-start | bytes 4194304 | tf_op jit(solution)/shard_map/all_to_all | solution.py:90
  112.8 10.4 %reshape.159 = bf16[64,1,16384]{2,1,0:T(2,128)(2,1)} reshape(bf16[64,2,8192]{2,1,0:T(2,128)(2,1)} %copy-done.1) | data formatting | bytes 4194304
  123.2 4.5 %convolution_convert_fusion.2 = bf16[8,16384]{1,0:T(8,128)(2,1)S(1)} fusion(bf16[64,1,16384]{2,1,0:T(2,128)(2,1)} %reshape.159, s32[64,8]{0,1:T(8,128)S(1)} %convert_reduce_fusion.1), kind=kOutput, calls=%fused_computation.5 | convolution fusion | flops 16908800 | bytes 2361344 | tf_op jit(solution)/shard_map/dot_general | solution.py:127
  128.6 12.8 %all_gather.14 = bf16[512,512]{1,0:T(8,128)(2,1)} all-gather(bf16[512,128]{1,0:T(8,128)(2,1)S(1)} %copy-done.3), channel_id=1, replica_groups=mesh['patch_0'=8,'patch_1'=4,'patch_2'=2,'mp'=4] {'mp'}, dimensions={1}, use_global_device_ids=true | all-gather | bytes 655360 | tf_op jit(solution)/shard_map/all_gather | solution.py:139
  141.3 2.5 convolution_multiply_fusion.3
  143.8 12.4 %all-gather.3.cloned.1.call-done = bf16[1024,512]{1,0:T(8,128)(2,1)} async-done(((bf16[1024,128]{1,0:T(8,128)(2,1)}), bf16[1024,512]{1,0:T(8,128)(2,1)}) %all-gather.3.cloned.1.call-update) | async-done | bytes 1048592 | tf_op jit(solution)/shard_map/all_gather | solution.py:138
  156.3 2.9 fusion.9
  159.2 71.2 %all-reduce.8.cloned.1.call-done = (f32[512,128]{0,1:T(8,128)}, f32[512,128]{1,0:T(8,128)}) async-done(((f32[512,128]{0,1:T(8,128)}, f32[512,128]{1,0:T(8,128)}), (f32[512,128]{0,1:T(8,128)}, f32[512,128]{1,0:T(8,128)})) %all-reduce.8.cloned.1.call-update) | async-done | bytes 524304 | tf_op jit(solution)/shard_map/psum | solution.py:35
  230.6 51.8 %all-reduce.10.cloned.1.call-done = (f32[512,128]{0,1:T(8,128)}, f32[512,128]{1,0:T(8,128)}) async-done(((f32[512,128]{0,1:T(8,128)}, f32[512,128]{1,0:T(8,128)}), (f32[512,128]{0,1:T(8,128)}, f32[512,128]{1,0:T(8,128)})) %all-reduce.10.cloned.1.call-update) | async-done | bytes 524304 | tf_op jit(solution)/shard_map/psum | solution.py:35
  282.6 6.7 %reshape.157 = bf16[64,1,16384]{2,1,0:T(2,128)(2,1)} reshape(bf16[64,2,8192]{2,1,0:T(2,128)(2,1)S(1)} %all-to-all-done) | data formatting | bytes 4194304
  289.3 4.5 %copy.66 = bf16[64,1,16384]{2,0,1:T(8,128)(2,1)S(1)} copy(bf16[64,1,16384]{2,1,0:T(2,128)(2,1)} %reshape.157) | data formatting | bytes 4194304
  298.0 20.0 %all-reduce.12.cloned.1.call-done = (f32[512,128]{0,1:T(8,128)}, f32[512,128]{1,0:T(8,128)}) async-done(((f32[512,128]{0,1:T(8,128)}, f32[512,128]{1,0:T(8,128)}), (f32[512,128]{0,1:T(8,128)}, f32[512,128]{1,0:T(8,128)})) %all-reduce.12.cloned.1.call-update) | async-done | bytes 524304 | tf_op jit(solution)/shard_map/psum | solution.py:35
  318.0 1.8 copy.52
  319.8 1.7 copy.76
  (62 shorter events, 19.8 us)
Async XLA Ops:
  7.2 48.1 %copy-start = (bf16[1024,512]{1,0:T(8,128)(2,1)S(1)}, bf16[1024,512]{1,0:T(8,128)(2,1)}, u32[]{:S(2)}) copy-start(bf16[1024,512]{1,0:T(8,128)(2,1)} %param.8) | copy-start | bytes 3145732
  7.9 29.8 %copy-start.8 = (f32[12]{0:T(128)}, f32[12]{0:T(128)S(1)}, u32[]{:S(2)}) copy-start(f32[12]{0:T(128)S(1)} %convert_element_type.60) | copy-start | bytes 148
  36.1 5.2 %copy-start.6 = (s32[12]{0:T(128)}, s32[12]{0:T(128)S(1)}, u32[]{:S(2)}) copy-start(s32[12]{0:T(128)S(1)} %add_reduce_fusion) | copy-start | bytes 148
  45.7 58.9 %all-to-all-start.1 = ((bf16[64,2,8192]{2,1,0:T(2,128)(2,1)}), bf16[64,2,8192]{2,1,0:T(2,128)(2,1)S(1)}, u32[]{:S(2)}, u32[]{:S(2)}) async-start(bf16[64,2,8192]{2,1,0:T(2,128)(2,1)} %reshape.158), calls=%async_computation.1 | async-start | bytes 4194304 | tf_op jit(solution)/shard_map/all_to_all | solution.py:120
  55.3 4.3 %copy-start.3 = (bf16[512,128]{1,0:T(8,128)(2,1)S(1)}, bf16[512,128]{1,0:T(8,128)(2,1)}, u32[]{:S(2)}) copy-start(bf16[512,128]{1,0:T(8,128)(2,1)} %param.14) | copy-start | bytes 393220
  58.6 1.0 copy-start.2
  104.6 1.4 copy-start.1
  106.0 176.6 %all-to-all-start = ((bf16[64,2,8192]{2,1,0:T(2,128)(2,1)}), bf16[64,2,8192]{2,1,0:T(2,128)(2,1)S(1)}, u32[]{:S(2)}, u32[]{:S(2)}) async-start(bf16[64,2,8192]{2,1,0:T(2,128)(2,1)} %reshape.156), calls=%async_computation | async-start | bytes 4194304 | tf_op jit(solution)/shard_map/all_to_all | solution.py:90
  112.8 43.5 %all-gather.3.cloned.1.call-start = ((), (), s32[]{:S(2)}) async-start(), calls=%async_computation.2 | async-start | bytes 1310720 | tf_op jit(solution)/shard_map/all_gather | solution.py:138
  128.5 101.9 %all-reduce.8.cloned.1.call-start = ((), (), s32[]{:S(2)}) async-start(), calls=%async_computation.3 | async-start | bytes 1048576 | tf_op jit(solution)/shard_map/psum | solution.py:35
  156.3 74.3 %copy-start.7 = (s32[12]{0:T(128)S(1)}, s32[12]{0:T(128)}, u32[]{:S(2)}) copy-start(s32[12]{0:T(128)} %copy-done.6) | copy-start | bytes 148
  156.3 126.2 %copy-start.5 = (bf16[128,128]{1,0:T(8,128)(2,1)S(1)}, bf16[128,128]{1,0:T(8,128)(2,1)}, u32[]{:S(2)}) copy-start(bf16[128,128]{1,0:T(8,128)(2,1)} %param.9) | copy-start | bytes 98308
  159.2 123.2 %all-reduce.10.cloned.1.call-start = ((), (), s32[]{:S(2)}) async-start(), calls=%async_computation.4 | async-start | bytes 1048576 | tf_op jit(solution)/shard_map/psum | solution.py:35
  230.5 87.5 %all-reduce.12.cloned.1.call-start = ((), (), s32[]{:S(2)}) async-start(), calls=%async_computation.5 | async-start | bytes 1048576 | tf_op jit(solution)/shard_map/psum | solution.py:35
  295.3 1.5 copy-start.4
  295.3 1.5 copy-start.9
Sparse Core Ops, SparseCore 0:
  128.7 27.5 all-gather.2
  159.3 71.1 all-reduce.7
  232.9 49.4 all-reduce.9
  284.9 33.0 all-reduce.11
where the time goes:
time: 329 us; the launch traced here: 328 us
  waiting for transfers between devices  186 us (57%)
  local copies, waits for them, and re-layouts  46 us (14%)
  blocking collectives  33.7 us (10%)
  matrix products  19.9 us (6%)
  starting transfers between devices  15.8 us (5%)
  between operations  14.6 us (4%)
  other arithmetic  12 us (4%)
    psum x3, waiting for transfers between devices, one_axis_at_a_time(): return functools.reduce(lax.psum, axes, array)  143 us
    unnamed x36, local copies, waits for them, and re-layouts  41.5 us
    all_to_all x1, waiting for transfers between devices, per_device(): lax.all_to_all(returning.reshape(devices, slot_cap, block_width), PATCH_A...  30.3 us
    unnamed x1, blocking collectives  21 us
    all_gather x1, blocking collectives, per_device(): second_piece = lax.all_gather(mlp_second, 'mp', axis=1, tiled=True)  12.8 us
    all_gather x1, waiting for transfers between devices, per_device(): grad_piece = lax.all_gather(grad_message, 'mp', axis=1, tiled=True)  12.4 us
    all_to_all x1, starting transfers between devices, per_device(): lax.all_to_all(returning.reshape(devices, slot_cap, block_width), PATCH_A...  8.9 us
    all_to_all x1, starting transfers between devices, per_device(): lax.all_to_all(outgoing, PATCH_AXES, split_axis=0, concat_axis=0, tiled=T...  6.79 us
  transfers between devices with their start and end apart: 6, of which 5 were waited for; matrix products, arithmetic and copies ran while one was open for 17% of the time, Pallas kernels for 0%

commit v1 on v0

v1 whole, which is shorter than its diff:
```python
import functools
import math

import jax
import jax.numpy as jnp
from jax import lax
from jax.experimental import pallas as pl
from jax.experimental.pallas import tpu as pltpu
from jax.sharding import Mesh
from jax.sharding import PartitionSpec as P

PATCH = 128
PATCH_AXES = ("patch_0", "patch_1", "patch_2")
AXES = PATCH_AXES + ("mp",)
F32 = jnp.float32
BF16 = jnp.bfloat16


def dot(a, b, dims=((1,), (0,))):
    return lax.dot_general(a, b, (dims, ((), ())), preferred_element_type=F32)


def kernel(
    sizes,
    scaling,
    tab_ref,
    meta_ref,
    grid_ref,
    latent_ref,
    w_ref,
    first_ref,
    second_ref,
    cot_ref,
    mesh_out,
    first_out,
    second_out,
    slots,
    V,
    cotb,
    metab,
    second,
    slope,
    hidden,
    msg,
    vbig,
    vbig_t,
    c_send,
    c_recv,
    y_send,
    y_recv,
    y_own,
    z_send,
    z_recv,
    x_send,
    x_recv,
    gm,
    gpre,
    gc_send,
    gc_recv,
    g_own,
    gx_send,
    gx_recv,
    gz_send,
    gz_recv,
    gy_send,
    gy_recv,
    fin,
    w_s,
    w_r,
    sec_s,
    sec_r,
    cx_s,
    cx_r,
    cz_s,
    cz_r,
    cy_s,
    cy_r,
    cc_s,
    cc_r,
    fc_s,
    fc_r,
    fy_s,
    fy_r,
    fz_s,
    fz_r,
    fx_s,
    fx_r,
    gc_s,
    gc_r,
    gx_s,
    gx_r,
    gz_s,
    gz_r,
    gy_s,
    gy_r,
    ay_s,
    ay_r,
    az_s,
    az_r,
    ac_s,
    ac_r,
    loc,
):
    Z, Y, C, X = sizes
    NP = Z * Y * C
    R, D = grid_ref.shape
    H = first_ref.shape[1]
    F = second_ref.shape[1]
    PX = PATCH // X
    GPD = R // PATCH
    HC = D // 2
    z, y, c, x = (lax.axis_index(a) for a in AXES)
    oc = 1 - c
    sent = []

    def send(src, dst, ss, rs, **where):
        place = {"patch_0": z, "patch_1": y, "patch_2": c, "mp": x}
        place.update(where)
        copy = pltpu.make_async_remote_copy(
            src_ref=src,
            dst_ref=dst,
            send_sem=ss,
            recv_sem=rs,
            device_id=place,
            device_id_type=pl.DeviceIdType.MESH,
        )
        copy.start()
        sent.append((src, dst, ss, rs))

    def arrive(dst, rs):
        pltpu.make_async_copy(dst, dst, rs).wait()

    def step(i, k, n):
        return lax.rem(i + k, n)

    xf = pl.ds(pl.multiple_of(x * F, F), F)
    xp = pl.ds(pl.multiple_of(x * PX, PX), PX)

    own_cot = pltpu.make_async_copy(cot_ref.at[xp, :], cotb.at[c, y, z, :, xf], loc.at[0])
    own_cot.start()
    own_second = pltpu.make_async_copy(second_ref, second.at[:, xf], loc.at[1])
    own_second.start()
    own_meta = pltpu.make_async_copy(meta_ref, metab.at[c, y, z], loc.at[2])
    own_meta.start()
    for k in range(1, X):
        to = step(x, k, X)
        rows = pl.ds(pl.multiple_of(to * PX, PX), PX)
        send(cot_ref.at[rows, :], cotb.at[c, y, z, :, xf], cx_s.at[k - 1], cx_r.at[k - 1], mp=to)
    for k in range(1, X):
        to = step(x, k, X)
        send(second_ref, second.at[:, xf], sec_s.at[k - 1], sec_r.at[k - 1], mp=to)

    def pack(i, carry):
        c1, y1, z1 = i // (Y * Z), (i // Z) % Y, i % Z
        natural = (z1 * Y + y1) * 2 + c1
        block = w_ref[tab_ref[0, natural], xp, :]
        live = tab_ref[1, natural]
        slots[i] = (block.astype(F32) * live.astype(F32)).astype(BF16)
        return carry

    lax.fori_loop(0, NP, pack, 0)
    here = (c * Y + y) * Z + z
    own_slot = pltpu.make_async_copy(slots.at[here], V.at[here], loc.at[3])
    own_slot.start()

    def send_slot(j, carry):
        dz, dy, dc = j // (Y * 2), (j // 2) % Y, j % 2
        z1, y1, c1 = lax.rem(z + dz, Z), lax.rem(y + dy, Y), lax.rem(c + dc, 2)
        pltpu.make_async_remote_copy(
            src_ref=slots.at[(c1 * Y + y1) * Z + z1],
            dst_ref=V.at[here],
            send_sem=w_s,
            recv_sem=w_r,
            device_id={"patch_0": z1, "patch_1": y1, "patch_2": c1, "mp": x},
            device_id_type=pl.DeviceIdType.MESH,
        ).start()
        return carry

    lax.fori_loop(1, NP, send_slot, 0)

    own_cot.wait()
    own_meta.wait()
    for k in range(1, X):
        arrive(cotb.at[c, y, z, :, xf], cx_r.at[k - 1])
    for k in range(1, Z):
        to = step(z, k, Z)
        send(cotb.at[c, y, z], cotb.at[c, y, z], cz_s.at[0, k - 1], cz_r.at[0, k - 1], patch_0=to)
        send(metab.at[c, y, z], metab.at[c, y, z], cz_s.at[1, k - 1], cz_r.at[1, k - 1], patch_0=to)

    TR = PATCH

    def first_layer(i, carry):
        rows = pl.ds(pl.multiple_of(i * TR, TR), TR)
        pre = dot(grid_ref[rows, :], first_ref[...])
        s = jax.nn.sigmoid(pre)
        hidden[rows, :] = (pre * s).astype(BF16)
        slope[rows, :] = s * (1.0 + pre * (1.0 - s))
        return carry

    lax.fori_loop(0, R // TR, first_layer, 0)

    for k in range(1, Z):
        frm = step(z, Z - k, Z)
        arrive(cotb.at[c, y, frm], cz_r.at[0, k - 1])
        arrive(metab.at[c, y, frm], cz_r.at[1, k - 1])
    for k in range(1, Y):
        to = step(y, k, Y)
        send(cotb.at[c, y], cotb.at[c, y], cy_s.at[0, k - 1], cy_r.at[0, k - 1], patch_1=to)
        send(metab.at[c, y], metab.at[c, y], cy_s.at[1, k - 1], cy_r.at[1, k - 1], patch_1=to)

    own_second.wait()
    for k in range(1, X):
        frm = step(x, X - k, X)
        arrive(second.at[:, pl.ds(pl.multiple_of(frm * F, F), F)], sec_r.at[k - 1])

    def second_layer(i, carry):
        rows = pl.ds(pl.multiple_of(i * TR, TR), TR)
        msg[rows, :] = dot(hidden[rows, :], second[...]).astype(BF16)
        return carry

    lax.fori_loop(0, R // TR, second_layer, 0)

    for k in range(1, Y):
        frm = step(y, Y - k, Y)
        arrive(cotb.at[c, frm], cy_r.at[0, k - 1])
        arrive(metab.at[c, frm], cy_r.at[1, k - 1])
    send(cotb.at[c], cotb.at[c], cc_s.at[0], cc_r.at[0], patch_2=oc)
    send(metab.at[c], metab.at[c], cc_s.at[1], cc_r.at[1], patch_2=oc)
    arrive(metab.at[oc], cc_r.at[1])

    own_slot.wait()
    pltpu.make_async_remote_copy(
        src_ref=all_but_one(slots, NP),
        dst_ref=all_but_one(V, NP),
        send_sem=w_s,
        recv_sem=w_r,
        device_id={"patch_0": z, "patch_1": y, "patch_2": oc, "mp": x},
        device_id_type=pl.DeviceIdType.MESH,
    ).wait_recv()
    own_natural = (z * Y + y) * 2 + c
    lanes = lax.broadcasted_iota(jnp.int32, (Z, PATCH), 1)
    TC = Z * PX

    def spread(i, carry):
        meta = metab[i // Y, lax.rem(i, Y)].reshape(Z, PATCH)
        patch_of = jnp.sum(jnp.where(lanes == own_natural, meta, 0.0), axis=1, keepdims=True)
        patch_rows = jnp.broadcast_to(
            jnp.broadcast_to(patch_of, (Z, PATCH))[:, None, :], (Z, PX, PATCH)
        ).reshape(TC, PATCH)
        blocks = V[pl.ds(pl.multiple_of(i * Z, Z), Z)].reshape(TC, PATCH).astype(F32)
        rows = pl.ds(pl.multiple_of(i * TC, TC), TC)
        blocks_t = blocks.T
        patch_cols = patch_rows.T
        for g in range(GPD):
            vbig[rows, g * PATCH : (g + 1) * PATCH] = jnp.where(
                patch_rows == float(g), blocks, 0.0
            ).astype(BF16)
            vbig_t[g * PATCH : (g + 1) * PATCH, rows] = jnp.where(
                patch_cols == float(g), blocks_t, 0.0
            ).astype(BF16)
        return carry

    lax.fori_loop(0, C * Y, spread, 0)


    def contribution(core, yy):
        at = pl.multiple_of((core * Y + yy) * TC, TC)
        return dot(vbig[pl.ds(at, TC), :], msg[...])

    for k in range(1, Y + 1):
        yy = step(y, k % Y, Y)
        c_send[yy] = contribution(oc, yy).astype(BF16).reshape(Z, PX, D)
        send(c_send.at[yy], c_recv.at[yy], fc_s.at[k - 1], fc_r.at[k - 1], patch_2=oc)
    for k in range(1, Y + 1):
        yy = step(y, k % Y, Y)
        part = contribution(c, yy)
        arrive(c_recv.at[yy], fc_r.at[k - 1])
        part = part + c_recv[yy].astype(F32).reshape(TC, D)
        if k < Y:
            y_send[k - 1] = part.astype(BF16).reshape(Z, PX, D)
            send(y_send.at[k - 1], y_recv.at[k - 1], fy_s.at[k - 1], fy_r.at[k - 1], patch_1=yy)
        else:
            y_own[...] = part.reshape(Z, PX, D)

    arrive(cotb.at[oc], cc_r.at[0])

    def message_gradient(i, carry):
        rows = pl.ds(pl.multiple_of(i * TR, TR), TR)
        gm[rows, :] = dot(vbig_t[rows, :], cotb[...].reshape(NP * PX, D)).astype(BF16)
        return carry

    lax.fori_loop(0, GPD, message_gradient, 0)

    for k in range(1, Y):
        arrive(y_recv.at[k - 1], fy_r.at[k - 1])
    total = y_own[...]
    for k in range(1, Y):
        total = total + y_recv[k - 1].astype(F32)
    y_own[...] = total
    z_send[...] = total.astype(BF16)
    for k in range(1, Z):
        to = step(z, k, Z)
        send(z_send.at[to], z_recv.at[k - 1], fz_s.at[k - 1], fz_r.at[k - 1], patch_0=to)

    def halves(which, left_ref, right_ref):
        for core in (oc, c):
            cols = pl.ds(pl.multiple_of(core * HC, HC), HC)
            part = dot(left_ref[:, cols], right_ref[...], ((0,), (0,))) * scaling
            for q in range(X):
                piece = part[:, q * F : (q + 1) * F]
                if core is oc:
                    gc_send[which, q] = piece.astype(BF16)
                else:
                    g_own[which, q] = piece
            if core is oc:
                send(
                    gc_send.at[which],
                    gc_recv.at[which],
                    gc_s.at[which],
                    gc_r.at[which],
                    patch_2=oc,
                )

    def over_mp(which):
        arrive(gc_recv.at[which], gc_r.at[which])
        for k in range(1, X):
            to = step(x, k, X)
            gx_send[which, k - 1] = (g_own[which, to] + gc_recv[which, to].astype(F32)).astype(BF16)
            send(
                gx_send.at[which, k - 1],
                gx_recv.at[which, k - 1],
                gx_s.at[which, k - 1],
                gx_r.at[which, k - 1],
                mp=to,
            )
        g_own[which, x] = g_own[which, x] + gc_recv[which, x].astype(F32)

    halves(0, hidden, gm)

    def pre_gradient(i, carry):
        rows = pl.ds(pl.multiple_of(i * TR, TR), TR)
        back = dot(gm[rows, :], second[...], ((1,), (1,)))
        gpre[rows, :] = (back * slope[rows, :]).astype(BF16)
        return carry

    lax.fori_loop(0, R // TR, pre_gradient, 0)
    over_mp(0)

    total = y_own[z]
    for k in range(1, Z):
        arrive(z_recv.at[k - 1], fz_r.at[k - 1])
        total = total + z_recv[k - 1].astype(F32)
    for q in range(X):
        x_send[q] = total[:, q * F : (q + 1) * F]
    own_sum = pltpu.make_async_copy(x_send.at[x], x_recv.at[x], loc.at[0])
    own_sum.start()
    for k in range(1, X):
        to = step(x, k, X)
        send(x_send.at[to], x_recv.at[x], fx_s.at[k - 1], fx_r.at[k - 1], mp=to)

    halves(1, grid_ref, gpre)
    over_mp(1)

    own_sum.wait()
    for k in range(1, X):
        arrive(x_recv.at[step(x, X - k, X)], fx_r.at[k - 1])
    mesh_out[...] = (latent_ref[...].astype(F32) + x_recv[...].reshape(PATCH, F)).astype(BF16)

    NR = HC // (Z * Y)
    for which in range(2):
        total = g_own[which, x]
        for k in range(1, X):
            arrive(gx_recv.at[which, k - 1], gx_r.at[which, k - 1])
            total = total + gx_recv[which, k - 1].astype(F32)
        gz_send[:, :, which] = total.reshape(Z, Y, NR, F)
    for k in range(1, Z):
        to = step(z, k, Z)
        send(gz_send.at[to], gz_recv.at[k - 1], gz_s.at[k - 1], gz_r.at[k - 1], patch_0=to)
    total = gz_send[z]
    for k in range(1, Z):
        arrive(gz_recv.at[k - 1], gz_r.at[k - 1])
        total = total + gz_recv[k - 1]
    gy_send[...] = total
    for k in range(1, Y):
        to = step(y, k, Y)
        send(gy_send.at[to], gy_recv.at[k - 1], gy_s.at[k - 1], gy_r.at[k - 1], patch_1=to)
    total = gy_send[y]
    for k in range(1, Y):
        arrive(gy_recv.at[k - 1], gy_r.at[k - 1])
        total = total + gy_recv[k - 1]
    fin[c, z, y] = total
    for k in range(1, Y):
        to = step(y, k, Y)
        send(fin.at[c, z, y], fin.at[c, z, y], ay_s.at[k - 1], ay_r.at[k - 1], patch_1=to)
    for k in range(1, Y):
        arrive(fin.at[c, z, step(y, Y - k, Y)], ay_r.at[k - 1])
    for k in range(1, Z):
        to = step(z, k, Z)
        send(fin.at[c, z], fin.at[c, z], az_s.at[k - 1], az_r.at[k - 1], patch_0=to)
    for k in range(1, Z):
        arrive(fin.at[c, step(z, Z - k, Z)], az_r.at[k - 1])
    send(fin.at[c], fin.at[c], ac_s.at[0], ac_r.at[0], patch_2=oc)
    arrive(fin.at[oc], ac_r.at[0])
    for core in range(2):
        rows = slice(core * HC, (core + 1) * HC)
        second_out[rows, :] = fin[core, :, :, 0].reshape(HC, F)
        first_out[rows, :] = fin[core, :, :, 1].reshape(HC, F)

    pltpu.make_async_remote_copy(
        src_ref=all_but_one(slots, NP),
        dst_ref=all_but_one(V, NP),
        send_sem=w_s,
        recv_sem=w_r,
        device_id={"patch_0": z, "patch_1": y, "patch_2": oc, "mp": x},
        device_id_type=pl.DeviceIdType.MESH,
    ).wait_send()
    for src, dst, ss, rs in sent:
        pltpu.make_async_copy(src, src, ss).wait()


def all_but_one(ref, n):
    return ref.at[pl.ds(0, n - 1)]


def per_device(
    grid_latent,
    mesh_latent,
    edge_weight,
    block_source,
    block_live,
    mlp_first,
    mlp_second,
    mesh_cotangent,
):
    Z, Y, C = (lax.axis_size(a) for a in PATCH_AXES)
    X = lax.axis_size("mp")
    NP = Z * Y * C
    R, D = grid_latent.shape
    H = mlp_first.shape[1]
    F = mlp_second.shape[1]
    PX = PATCH // X
    GPD = R // PATCH
    HC = D // 2
    NR = HC // (Z * Y)
    slots_of = edge_weight.shape[0]
    hit = (block_source // GPD)[:, None] == jnp.arange(PATCH)[None, :]
    values = jnp.stack([jnp.arange(slots_of, dtype=jnp.int32), block_live, block_source % GPD])
    tab = jnp.sum(jnp.where(hit[None], values[:, :, None], 0), axis=1)
    meta = tab[2:3].astype(F32)
    scaling = 1.0 / math.sqrt(R * NP)

    vm = pltpu.VMEM
    dma = pltpu.SemaphoreType.DMA
    scratch = [
        vm((NP, PX, PATCH), BF16),
        vm((NP, PX, PATCH), BF16),
        vm((C, Y, Z, PX, D), BF16),
        vm((C, Y, Z, 1, PATCH), F32),
        vm((H, D), BF16),
        vm((R, H), F32),
        vm((R, H), BF16),
        vm((R, D), BF16),
        vm((NP * PX, R), BF16),
        vm((R, NP * PX), BF16),
        vm((Y, Z, PX, D), BF16),
        vm((Y, Z, PX, D), BF16),
        vm((Y - 1, Z, PX, D), BF16),
        vm((Y - 1, Z, PX, D), BF16),
        vm((Z, PX, D), F32),
        vm((Z, PX, D), BF16),
        vm((Z - 1, PX, D), BF16),
        vm((X, PX, F), F32),
        vm((X, PX, F), F32),
        vm((R, D), BF16),
        vm((R, H), BF16),
        vm((2, X, HC, F), BF16),
        vm((2, X, HC, F), BF16),
        vm((2, X, HC, F), F32),
        vm((2, X - 1, HC, F), BF16),
        vm((2, X - 1, HC, F), BF16),
        vm((Z, Y, 2, NR, F), F32),
        vm((Z - 1, Y, 2, NR, F), F32),
        vm((Y, 2, NR, F), F32),
        vm((Y - 1, 2, NR, F), F32),
        vm((C, Z, Y, 2, NR, F), F32),
        dma,
        dma,
        dma((X - 1,)),
        dma((X - 1,)),
        dma((X - 1,)),
        dma((X - 1,)),
        dma((2, Z - 1)),
        dma((2, Z - 1)),
        dma((2, Y - 1)),
        dma((2, Y - 1)),
        dma((2,)),
        dma((2,)),
        dma((Y,)),
        dma((Y,)),
        dma((Y - 1,)),
        dma((Y - 1,)),
        dma((Z - 1,)),
        dma((Z - 1,)),
        dma((X - 1,)),
        dma((X - 1,)),
        dma((2,)),
        dma((2,)),
        dma((2, X - 1)),
        dma((2, X - 1)),
        dma((Z - 1,)),
        dma((Z - 1,)),
        dma((Y - 1,)),
        dma((Y - 1,)),
        dma((Y - 1,)),
        dma((Y - 1,)),
        dma((Z - 1,)),
        dma((Z - 1,)),
        dma((1,)),
        dma((1,)),
        dma((4,)),
    ]
    in_vmem = pl.BlockSpec(memory_space=pltpu.VMEM)
    mesh_out, grad_first, grad_second = pl.pallas_call(
        functools.partial(kernel, (Z, Y, C, X), scaling),
        out_shape=(
            jax.ShapeDtypeStruct((PATCH, F), BF16),
            jax.ShapeDtypeStruct((D, F), F32),
            jax.ShapeDtypeStruct((H, F), F32),
        ),
        in_specs=[pl.BlockSpec(memory_space=pltpu.SMEM)] + [in_vmem] * 7,
        out_specs=(in_vmem, in_vmem, in_vmem),
        scratch_shapes=scratch,
        compiler_params=pltpu.CompilerParams(
            has_side_effects=True, vmem_limit_bytes=62 * 1024 * 1024
        ),
    )(
        tab,
        meta,
        grid_latent,
        mesh_latent,
        edge_weight,
        mlp_first,
        mlp_second,
        mesh_cotangent,
    )
    return mesh_out, grad_first, grad_second


def solution(mesh):
    mp = mesh.shape["mp"]
    cores = 2
    rows = mesh.shape["patch"] // cores
    depth = 8 if rows % 8 == 0 else 2
    torus = Mesh(mesh.devices.reshape(depth, rows // depth, cores, mp), AXES)
    in_specs = (
        P(PATCH_AXES, None),
        P(PATCH_AXES, "mp"),
        P(PATCH_AXES, None, None),
        P(PATCH_AXES),
        P(PATCH_AXES),
        P(),
        P(None, "mp"),
        P(PATCH_AXES, "mp"),
    )
    out_specs = (P(PATCH_AXES, "mp"), P(None, "mp"), P(None, "mp"))
    return jax.shard_map(
        per_device, mesh=torus, in_specs=in_specs, out_specs=out_specs, check_vma=False
    )
```

time: 329 us -> 125 us (0.38)
  waiting for transfers between devices: 186 us -> 0 us
  Pallas kernels: 0 us -> 119 us
  local copies, waits for them, and re-layouts: 46 us -> 5.07 us
  blocking collectives: 33.7 us -> 0 us
  matrix products: 19.9 us -> 0 us
  starting transfers between devices: 15.8 us -> 0 us
  between operations: 14.6 us -> 0.67 us
  other arithmetic: 12 us -> 0.7 us
    psum x3 -> x0, waiting for transfers between devices: 143 us -> none  [one_axis_at_a_time(): return functools.reduce(lax.psum, axes, array)]
    pallas_call x0 -> x1, Pallas kernels: none -> 119 us  [per_device(): pl.pallas_call(functools.partial(kernel, (Z, Y, C, X), scaling), out_shap...]
    unnamed x36 -> x11, local copies, waits for them, and re-layouts: 41.5 us -> 5.07 us
    all_to_all x2 -> x0, waiting for transfers between devices: 30.3 us -> none  [the longest x1 30.3 us: per_device(): lax.all_to_all(returning.reshape(devices, slot_cap, block_width), PATCH_A...]
    unnamed x1 -> x0, blocking collectives: 21 us -> none
    dot_general x9 -> x0, matrix products: 19.9 us -> none  [the longest x1 4.48 us: per_device(): lax.dot_general(picking, back_flat, (((0,), (0,)), ((), ())), preferred_e...]
    all_to_all x2 -> x0, starting transfers between devices: 15.7 us -> none  [the longest x1 8.9 us: per_device(): lax.all_to_all(returning.reshape(devices, slot_cap, block_width), PATCH_A...]
    all_gather x1 -> x0, blocking collectives: 12.8 us -> none  [per_device(): second_piece = lax.all_gather(mlp_second, 'mp', axis=1, tiled=True)]
  transfers between devices with their start and end apart: 6 -> 0, of which waited for: 5 -> 0; matrix products, arithmetic and copies ran while one was open for 17% -> 0% of each run, Pallas kernels for 0% -> 0%
where the time goes in v1:
time: 125 us
  Pallas kernels  119 us (95%)
  local copies, waits for them, and re-layouts  5.07 us (4%)
    pallas_call x1, Pallas kernels, per_device(): pl.pallas_call(functools.partial(kernel, (Z, Y, C, X), scaling), out_shap...  119 us
    unnamed x11, local copies, waits for them, and re-layouts  5.07 us

profile of v1, /device:TPU:1, one launch (start us, length us, event | category | flops | bytes accessed | tf_op | source)
XLA Modules:
  0.0 125.2 jit_solution(5804008489035030950)
XLA Ops:
  0.6 0.0 copy-start.3
  0.7 0.6 copy-done.3
  1.3 0.0 copy-start.2
  1.3 0.1 iota_compare_fusion
  1.4 0.6 copy-done.2
  2.0 0.1 select_reduce_fusion.tab_ref
  2.1 0.0 copy-start.1
  2.1 0.5 slice_convert_fusion.meta_ref
  2.6 0.1 copy-done.1
  2.6 118.8 %shard_map.103 = (bf16[128,128]{1,0:T(8,128)(2,1)}, f32[512,128]{1,0:T(8,128)}, f32[512,128]{1,0:T(8,128)}) custom-call(s32[3,128]{1,0:T(4,128)} %copy-done.1, f32[1,128]{1,0:T(1,128)} %slice_convert_fusion.meta_ref, bf16[1024,512]{1,0:T(8,128)(2,1)} %grid_ref.1, bf16[128,128]{1,0:T(8,128)(2,1)} %latent_ref.1, bf16[12,128,128]{2,1,0:T(8,128)(2,1)} %w_ref.1, ...), custom_call_target="tpu_custom_call" | custom-call | tf_op jit(solution)/shard_map/pallas_call | solution.py:523
  121.4 1.4 %copy.14 = bf16[128,128]{1,0:T(8,128)(2,1)} copy(bf16[128,128]{1,0:T(8,128)(2,1)} %get-tuple-element.8) | data formatting | bytes 65536
  122.8 0.0 copy-start
  122.8 1.7 %copy.15 = f32[512,128]{1,0:T(8,128)} copy(f32[512,128]{1,0:T(8,128)} %get-tuple-element.9) | data formatting | bytes 524288
  124.5 0.0 copy-done
  124.5 0.7 copy.16
  (3 shorter events, 0.0 us)
Async XLA Ops:
  0.6 0.7 copy-start.3
  1.3 0.7 copy-start.2
  2.1 0.6 copy-start.1
  122.8 1.7 %copy-start = (f32[512,128]{1,0:T(8,128)S(1)}, f32[512,128]{1,0:T(8,128)}, u32[]{:S(2)}) copy-start(f32[512,128]{1,0:T(8,128)} %get-tuple-element.10) | copy-start | bytes 786436

commit v2 on v1

--- a/solution.py
+++ b/solution.py
@@ -25,15 +25,21 @@
     scaling,
     tab_ref,
     meta_ref,
+    grid_in,
+    latent_in,
+    w_in,
+    first_in,
+    second_in,
+    cot_in,
+    mesh_out,
+    first_out,
+    second_out,
     grid_ref,
     latent_ref,
     w_ref,
     first_ref,
     second_ref,
     cot_ref,
-    mesh_out,
-    first_out,
-    second_out,
     slots,
     V,
     cotb,
@@ -62,8 +68,8 @@
     gx_recv,
     gz_send,
     gz_recv,
-    gy_send,
-    gy_recv,
+    gy,
+    own,
     fin,
     w_s,
     w_r,
@@ -93,19 +99,18 @@
     gz_r,
     gy_s,
     gy_r,
-    ay_s,
-    ay_r,
     az_s,
     az_r,
     ac_s,
     ac_r,
     loc,
+    load_s,
 ):
     Z, Y, C, X = sizes
     NP = Z * Y * C
-    R, D = grid_ref.shape
-    H = first_ref.shape[1]
-    F = second_ref.shape[1]
+    R, D = grid_in.shape
+    H = first_in.shape[1]
+    F = second_in.shape[1]
     PX = PATCH // X
     GPD = R // PATCH
     HC = D // 2
@@ -136,16 +141,59 @@
     xf = pl.ds(pl.multiple_of(x * F, F), F)
     xp = pl.ds(pl.multiple_of(x * PX, PX), PX)
 
+    loads = {}
+    for i, (name, src, dst) in enumerate(
+        (
+            ("cot", cot_in, cot_ref),
+            ("w", w_in, w_ref),
+            ("second", second_in, second_ref),
+            ("grid", grid_in, grid_ref),
+            ("first", first_in, first_ref),
+            ("latent", latent_in, latent_ref),
+        )
+    ):
+        loads[name] = pltpu.make_async_copy(src, dst, load_s.at[i])
+        loads[name].start()
+
+    barrier = pltpu.get_barrier_semaphore()
+
+    def greet(j, carry):
+        dz, dy, dc = j // (Y * 2), (j // 2) % Y, j % 2
+        pl.semaphore_signal(
+            barrier,
+            inc=1,
+            device_id={
+                "patch_0": lax.rem(z + dz, Z),
+                "patch_1": lax.rem(y + dy, Y),
+                "patch_2": lax.rem(c + dc, 2),
+                "mp": x,
+            },
+            device_id_type=pl.DeviceIdType.MESH,
+        )
+        return carry
+
+    for k in range(1, X):
+        pl.semaphore_signal(
+            barrier,
+            inc=1,
+            device_id={"patch_0": z, "patch_1": y, "patch_2": c, "mp": step(x, k, X)},
+            device_id_type=pl.DeviceIdType.MESH,
+        )
+    lax.fori_loop(1, NP, greet, 0)
+    loads["cot"].wait()
+    pl.semaphore_wait(barrier, NP - 1 + X - 1)
+
     own_cot = pltpu.make_async_copy(cot_ref.at[xp, :], cotb.at[c, y, z, :, xf], loc.at[0])
     own_cot.start()
-    own_second = pltpu.make_async_copy(second_ref, second.at[:, xf], loc.at[1])
-    own_second.start()
     own_meta = pltpu.make_async_copy(meta_ref, metab.at[c, y, z], loc.at[2])
     own_meta.start()
     for k in range(1, X):
         to = step(x, k, X)
         rows = pl.ds(pl.multiple_of(to * PX, PX), PX)
         send(cot_ref.at[rows, :], cotb.at[c, y, z, :, xf], cx_s.at[k - 1], cx_r.at[k - 1], mp=to)
+    loads["second"].wait()
+    own_second = pltpu.make_async_copy(second_ref, second.at[:, xf], loc.at[1])
+    own_second.start()
     for k in range(1, X):
         to = step(x, k, X)
         send(second_ref, second.at[:, xf], sec_s.at[k - 1], sec_r.at[k - 1], mp=to)
@@ -158,7 +206,18 @@
         slots[i] = (block.astype(F32) * live.astype(F32)).astype(BF16)
         return carry
 
+    loads["w"].wait()
     lax.fori_loop(0, NP, pack, 0)
+
+    own_cot.wait()
+    own_meta.wait()
+    for k in range(1, X):
+        arrive(cotb.at[c, y, z, :, xf], cx_r.at[k - 1])
+    for k in range(1, Z):
+        to = step(z, k, Z)
+        send(cotb.at[c, y, z], cotb.at[c, y, z], cz_s.at[0, k - 1], cz_r.at[0, k - 1], patch_0=to)
+        send(metab.at[c, y, z], metab.at[c, y, z], cz_s.at[1, k - 1], cz_r.at[1, k - 1], patch_0=to)
+
     here = (c * Y + y) * Z + z
     own_slot = pltpu.make_async_copy(slots.at[here], V.at[here], loc.at[3])
     own_slot.start()
@@ -178,16 +237,9 @@
 
     lax.fori_loop(1, NP, send_slot, 0)
 
-    own_cot.wait()
-    own_meta.wait()
-    for k in range(1, X):
-        arrive(cotb.at[c, y, z, :, xf], cx_r.at[k - 1])
-    for k in range(1, Z):
-        to = step(z, k, Z)
-        send(cotb.at[c, y, z], cotb.at[c, y, z], cz_s.at[0, k - 1], cz_r.at[0, k - 1], patch_0=to)
-        send(metab.at[c, y, z], metab.at[c, y, z], cz_s.at[1, k - 1], cz_r.at[1, k - 1], patch_0=to)
-
     TR = PATCH
+    loads["grid"].wait()
+    loads["first"].wait()
 
     def first_layer(i, carry):
         rows = pl.ds(pl.multiple_of(i * TR, TR), TR)
@@ -203,10 +255,13 @@
         frm = step(z, Z - k, Z)
         arrive(cotb.at[c, y, frm], cz_r.at[0, k - 1])
         arrive(metab.at[c, y, frm], cz_r.at[1, k - 1])
+    ring = Y == 4
+    up, down, across = step(y, 1, Y), step(y, Y - 1, Y), step(y, 2, Y)
     for k in range(1, Y):
         to = step(y, k, Y)
-        send(cotb.at[c, y], cotb.at[c, y], cy_s.at[0, k - 1], cy_r.at[0, k - 1], patch_1=to)
         send(metab.at[c, y], metab.at[c, y], cy_s.at[1, k - 1], cy_r.at[1, k - 1], patch_1=to)
+        if not ring or k != 2:
+            send(cotb.at[c, y], cotb.at[c, y], cy_s.at[0, k - 1], cy_r.at[0, k - 1], patch_1=to)
 
     own_second.wait()
     for k in range(1, X):
@@ -222,9 +277,19 @@
 
     for k in range(1, Y):
         frm = step(y, Y - k, Y)
-        arrive(cotb.at[c, frm], cy_r.at[0, k - 1])
         arrive(metab.at[c, frm], cy_r.at[1, k - 1])
-    send(cotb.at[c], cotb.at[c], cc_s.at[0], cc_r.at[0], patch_2=oc)
+        if not ring or k != 2:
+            arrive(cotb.at[c, frm], cy_r.at[0, k - 1])
+    if ring:
+        for i, (frm, to) in enumerate(((down, up), (up, down))):
+            half = pl.ds(i * (Z // 2), Z // 2)
+            send(
+                cotb.at[c, frm, half],
+                cotb.at[c, frm, half],
+                cy_s.at[i, Y - 1],
+                cy_r.at[i, Y - 1],
+                patch_1=to,
+            )
     send(metab.at[c], metab.at[c], cc_s.at[1], cc_r.at[1], patch_2=oc)
     arrive(metab.at[oc], cc_r.at[1])
 
@@ -271,6 +336,10 @@
         yy = step(y, k % Y, Y)
         c_send[yy] = contribution(oc, yy).astype(BF16).reshape(Z, PX, D)
         send(c_send.at[yy], c_recv.at[yy], fc_s.at[k - 1], fc_r.at[k - 1], patch_2=oc)
+    if ring:
+        for i in range(2):
+            arrive(cotb.at[c, across, pl.ds(i * (Z // 2), Z // 2)], cy_r.at[i, Y - 1])
+    send(cotb.at[c], cotb.at[c], cc_s.at[0], cc_r.at[0], patch_2=oc)
     for k in range(1, Y + 1):
         yy = step(y, k % Y, Y)
         part = contribution(c, yy)
@@ -291,17 +360,6 @@
 
     lax.fori_loop(0, GPD, message_gradient, 0)
 
-    for k in range(1, Y):
-        arrive(y_recv.at[k - 1], fy_r.at[k - 1])
-    total = y_own[...]
-    for k in range(1, Y):
-        total = total + y_recv[k - 1].astype(F32)
-    y_own[...] = total
-    z_send[...] = total.astype(BF16)
-    for k in range(1, Z):
-        to = step(z, k, Z)
-        send(z_send.at[to], z_recv.at[k - 1], fz_s.at[k - 1], fz_r.at[k - 1], patch_0=to)
-
     def halves(which, left_ref, right_ref):
         for core in (oc, c):
             cols = pl.ds(pl.multiple_of(core * HC, HC), HC)
@@ -309,7 +367,7 @@
             for q in range(X):
                 piece = part[:, q * F : (q + 1) * F]
                 if core is oc:
-                    gc_send[which, q] = piece.astype(BF16)
+                    gc_send[which, q] = piece
                 else:
                     g_own[which, q] = piece
             if core is oc:
@@ -325,7 +383,7 @@
         arrive(gc_recv.at[which], gc_r.at[which])
         for k in range(1, X):
             to = step(x, k, X)
-            gx_send[which, k - 1] = (g_own[which, to] + gc_recv[which, to].astype(F32)).astype(BF16)
+            gx_send[which, k - 1] = (g_own[which, to] + gc_recv[which, to]).astype(BF16)
             send(
                 gx_send.at[which, k - 1],
                 gx_recv.at[which, k - 1],
@@ -333,7 +391,7 @@
                 gx_r.at[which, k - 1],
                 mp=to,
             )
-        g_own[which, x] = g_own[which, x] + gc_recv[which, x].astype(F32)
+        g_own[which, x] = g_own[which, x] + gc_recv[which, x]
 
     halves(0, hidden, gm)
 
@@ -345,6 +403,33 @@
 
     lax.fori_loop(0, R // TR, pre_gradient, 0)
     over_mp(0)
+
+    halves(1, grid_ref, gpre)
+
+    for k in range(1, Y):
+        arrive(y_recv.at[k - 1], fy_r.at[k - 1])
+    total = y_own[...]
+    for k in range(1, Y):
+        total = total + y_recv[k - 1].astype(F32)
+    y_own[...] = total
+    z_send[...] = total.astype(BF16)
+    for k in range(1, Z):
+        to = step(z, k, Z)
+        send(z_send.at[to], z_recv.at[k - 1], fz_s.at[k - 1], fz_r.at[k - 1], patch_0=to)
+
+    over_mp(1)
+
+    ZR = HC // Z
+    for which in range(2):
+        total = g_own[which, x]
+        for k in range(1, X):
+            arrive(gx_recv.at[which, k - 1], gx_r.at[which, k - 1])
+            total = total + gx_recv[which, k - 1].astype(F32)
+        g_own[which, x] = total
+        gz_send[:, which] = total.reshape(Z, ZR, F).astype(BF16)
+    for k in range(1, Z):
+        to = step(z, k, Z)
+        send(gz_send.at[to], gz_recv.at[k - 1], gz_s.at[k - 1], gz_r.at[k - 1], patch_0=to)
 
     total = y_own[z]
     for k in range(1, Z):
@@ -358,53 +443,39 @@
         to = step(x, k, X)
         send(x_send.at[to], x_recv.at[x], fx_s.at[k - 1], fx_r.at[k - 1], mp=to)
 
-    halves(1, grid_ref, gpre)
-    over_mp(1)
+    total = g_own[:, x, pl.ds(pl.multiple_of(z * ZR, ZR), ZR)]
+    for k in range(1, Z):
+        arrive(gz_recv.at[k - 1], gz_r.at[k - 1])
+        total = total + gz_recv[k - 1].astype(F32)
+    gy[y] = total
+    for k in range(1, Y):
+        to = step(y, k, Y)
+        send(gy.at[y], gy.at[y], gy_s.at[k - 1], gy_r.at[k - 1], patch_1=to)
 
     own_sum.wait()
     for k in range(1, X):
         arrive(x_recv.at[step(x, X - k, X)], fx_r.at[k - 1])
+    loads["latent"].wait()
     mesh_out[...] = (latent_ref[...].astype(F32) + x_recv[...].reshape(PATCH, F)).astype(BF16)
 
-    NR = HC // (Z * Y)
-    for which in range(2):
-        total = g_own[which, x]
-        for k in range(1, X):
-            arrive(gx_recv.at[which, k - 1], gx_r.at[which, k - 1])
-            total = total + gx_recv[which, k - 1].astype(F32)
-        gz_send[:, :, which] = total.reshape(Z, Y, NR, F)
+    for k in range(1, Y):
+        arrive(gy.at[step(y, Y - k, Y)], gy_r.at[k - 1])
+    total = gy[0]
+    for yy in range(1, Y):
+        total = total + gy[yy]
+    own[...] = total.astype(BF16)
     for k in range(1, Z):
         to = step(z, k, Z)
-        send(gz_send.at[to], gz_recv.at[k - 1], gz_s.at[k - 1], gz_r.at[k - 1], patch_0=to)
-    total = gz_send[z]
-    for k in range(1, Z):
-        arrive(gz_recv.at[k - 1], gz_r.at[k - 1])
-        total = total + gz_recv[k - 1]
-    gy_send[...] = total
-    for k in range(1, Y):
-        to = step(y, k, Y)
-        send(gy_send.at[to], gy_recv.at[k - 1], gy_s.at[k - 1], gy_r.at[k - 1], patch_1=to)
-    total = gy_send[y]
-    for k in range(1, Y):
-        arrive(gy_recv.at[k - 1], gy_r.at[k - 1])
-        total = total + gy_recv[k - 1]
-    fin[c, z, y] = total
-    for k in range(1, Y):
-        to = step(y, k, Y)
-        send(fin.at[c, z, y], fin.at[c, z, y], ay_s.at[k - 1], ay_r.at[k - 1], patch_1=to)
-    for k in range(1, Y):
-        arrive(fin.at[c, z, step(y, Y - k, Y)], ay_r.at[k - 1])
-    for k in range(1, Z):
-        to = step(z, k, Z)
-        send(fin.at[c, z], fin.at[c, z], az_s.at[k - 1], az_r.at[k - 1], patch_0=to)
+        send(own, fin.at[c, z], az_s.at[k - 1], az_r.at[k - 1], patch_0=to)
+    fin[c, z] = own[...]
     for k in range(1, Z):
         arrive(fin.at[c, step(z, Z - k, Z)], az_r.at[k - 1])
     send(fin.at[c], fin.at[c], ac_s.at[0], ac_r.at[0], patch_2=oc)
     arrive(fin.at[oc], ac_r.at[0])
     for core in range(2):
         rows = slice(core * HC, (core + 1) * HC)
-        second_out[rows, :] = fin[core, :, :, 0].reshape(HC, F)
-        first_out[rows, :] = fin[core, :, :, 1].reshape(HC, F)
+        second_out[rows, :] = fin[core, :, 0].reshape(HC, F).astype(F32)
+        first_out[rows, :] = fin[core, :, 1].reshape(HC, F).astype(F32)
 
     pltpu.make_async_remote_copy(
         src_ref=all_but_one(slots, NP),
@@ -441,7 +512,7 @@
     PX = PATCH // X
     GPD = R // PATCH
     HC = D // 2
-    NR = HC // (Z * Y)
+    ZR = HC // Z
     slots_of = edge_weight.shape[0]
     hit = (block_source // GPD)[:, None] == jnp.arange(PATCH)[None, :]
     values = jnp.stack([jnp.arange(slots_of, dtype=jnp.int32), block_live, block_source % GPD])
@@ -452,6 +523,12 @@
     vm = pltpu.VMEM
     dma = pltpu.SemaphoreType.DMA
     scratch = [
+        vm(grid_latent.shape, BF16),
+        vm(mesh_latent.shape, BF16),
+        vm(edge_weight.shape, BF16),
+        vm(mlp_first.shape, BF16),
+        vm(mlp_second.shape, BF16),
+        vm(mesh_cotangent.shape, BF16),
         vm((NP, PX, PATCH), BF16),
         vm((NP, PX, PATCH), BF16),
         vm((C, Y, Z, PX, D), BF16),
@@ -473,16 +550,16 @@
         vm((X, PX, F), F32),
         vm((R, D), BF16),
         vm((R, H), BF16),
-        vm((2, X, HC, F), BF16),
-        vm((2, X, HC, F), BF16),
+        vm((2, X, HC, F), F32),
+        vm((2, X, HC, F), F32),
         vm((2, X, HC, F), F32),
         vm((2, X - 1, HC, F), BF16),
         vm((2, X - 1, HC, F), BF16),
-        vm((Z, Y, 2, NR, F), F32),
-        vm((Z - 1, Y, 2, NR, F), F32),
-        vm((Y, 2, NR, F), F32),
-        vm((Y - 1, 2, NR, F), F32),
-        vm((C, Z, Y, 2, NR, F), F32),
+        vm((Z, 2, ZR, F), BF16),
+        vm((Z - 1, 2, ZR, F), BF16),
+        vm((Y, 2, ZR, F), F32),
+        vm((2, ZR, F), BF16),
+        vm((C, Z, 2, ZR, F), BF16),
         dma,
         dma,
         dma((X - 1,)),
@@ -491,8 +568,8 @@
         dma((X - 1,)),
         dma((2, Z - 1)),
         dma((2, Z - 1)),
-        dma((2, Y - 1)),
-        dma((2, Y - 1)),
+        dma((2, Y)),
+        dma((2, Y)),
         dma((2,)),
         dma((2,)),
         dma((Y,)),
@@ -511,13 +588,12 @@
         dma((Z - 1,)),
         dma((Y - 1,)),
         dma((Y - 1,)),
-        dma((Y - 1,)),
-        dma((Y - 1,)),
         dma((Z - 1,)),
         dma((Z - 1,)),
         dma((1,)),
         dma((1,)),
         dma((4,)),
+        dma((6,)),
     ]
     in_vmem = pl.BlockSpec(memory_space=pltpu.VMEM)
     mesh_out, grad_first, grad_second = pl.pallas_call(
@@ -527,11 +603,12 @@
             jax.ShapeDtypeStruct((D, F), F32),
             jax.ShapeDtypeStruct((H, F), F32),
         ),
-        in_specs=[pl.BlockSpec(memory_space=pltpu.SMEM)] + [in_vmem] * 7,
+        in_specs=[pl.BlockSpec(memory_space=pltpu.SMEM), in_vmem]
+        + [pl.BlockSpec(memory_space=pl.ANY)] * 6,
         out_specs=(in_vmem, in_vmem, in_vmem),
         scratch_shapes=scratch,
         compiler_params=pltpu.CompilerParams(
-            has_side_effects=True, vmem_limit_bytes=62 * 1024 * 1024
+            collective_id=0, has_side_effects=True, vmem_limit_bytes=62 * 1024 * 1024
         ),
     )(
         tab,

time: 125 us -> 89.6 us (0.72)
  Pallas kernels: 119 us -> 83 us
    pallas_call x1, Pallas kernels: 119 us -> 83 us  [per_device(): pl.pallas_call(functools.partial(kernel, (Z, Y, C, X), scaling), out_shap...]
where the time goes in v2:
time: 89.6 us; the launch traced here: 89.4 us
  Pallas kernels  83 us (93%)
  local copies, waits for them, and re-layouts  5.07 us (6%)
    pallas_call x1, Pallas kernels, per_device(): pl.pallas_call(functools.partial(kernel, (Z, Y, C, X), scaling), out_shap...  83 us
    unnamed x11, local copies, waits for them, and re-layouts  5.07 us

profile of v2, /device:TPU:1, one launch (start us, length us, event | category | flops | bytes accessed | tf_op | source)
XLA Modules:
  0.0 89.4 jit_solution(10400355385017746698)
XLA Ops:
  0.6 0.0 copy-start.3
  0.7 0.6 copy-done.3
  1.3 0.0 copy-start.2
  1.3 0.1 iota_compare_fusion
  1.4 0.6 copy-done.2
  2.0 0.1 select_reduce_fusion.tab_ref
  2.1 0.0 copy-start.1
  2.1 0.5 slice_convert_fusion.meta_ref
  2.6 0.1 copy-done.1
  2.6 83.0 %shard_map.103 = (bf16[128,128]{1,0:T(8,128)(2,1)}, f32[512,128]{1,0:T(8,128)}, f32[512,128]{1,0:T(8,128)}) custom-call(s32[3,128]{1,0:T(4,128)} %copy-done.1, f32[1,128]{1,0:T(1,128)} %slice_convert_fusion.meta_ref, bf16[1024,512]{1,0:T(8,128)(2,1)} %grid_in.1, bf16[128,128]{1,0:T(8,128)(2,1)} %latent_in.1, bf16[12,128,128]{2,1,0:T(8,128)(2,1)} %w_in.1, ...), custom_call_target="tpu_custom_call" | custom-call | tf_op jit(solution)/shard_map/pallas_call | solution.py:599
  85.6 1.4 %copy.14 = bf16[128,128]{1,0:T(8,128)(2,1)} copy(bf16[128,128]{1,0:T(8,128)(2,1)} %get-tuple-element.8) | data formatting | bytes 65536
  87.0 0.0 copy-start
  87.0 1.7 %copy.15 = f32[512,128]{1,0:T(8,128)} copy(f32[512,128]{1,0:T(8,128)} %get-tuple-element.9) | data formatting | bytes 524288
  88.7 0.0 copy-done
  88.7 0.7 copy.16
  (3 shorter events, 0.0 us)
Async XLA Ops:
  0.6 0.7 copy-start.3
  1.3 0.7 copy-start.2
  2.1 0.6 copy-start.1
  87.0 1.7 %copy-start = (f32[512,128]{1,0:T(8,128)S(1)}, f32[512,128]{1,0:T(8,128)}, u32[]{:S(2)}) copy-start(f32[512,128]{1,0:T(8,128)} %get-tuple-element.10) | copy-start | bytes 786436

commit v3 on v2

--- a/solution.py
+++ b/solution.py
@@ -23,8 +23,8 @@
 def kernel(
     sizes,
     scaling,
-    tab_ref,
-    meta_ref,
+    source_ref,
+    live_ref,
     grid_in,
     latent_in,
     w_in,
@@ -34,6 +34,7 @@
     mesh_out,
     first_out,
     second_out,
+    meta_ref,
     grid_ref,
     latent_ref,
     w_ref,
@@ -81,8 +82,16 @@
     cz_r,
     cy_s,
     cy_r,
+    ch_s,
+    ch_r,
     cc_s,
     cc_r,
+    mz_s,
+    mz_r,
+    my_s,
+    my_r,
+    mc_s,
+    mc_r,
     fc_s,
     fc_r,
     fy_s,
@@ -180,47 +189,53 @@
             device_id_type=pl.DeviceIdType.MESH,
         )
     lax.fori_loop(1, NP, greet, 0)
+
+    n_slots = w_in.shape[0]
+
+    def feeder(j):
+        return jnp.where(live_ref[j] == 1, lax.div(source_ref[j], GPD), -1)
+
+    lane = lax.broadcasted_iota(jnp.int32, (1, PATCH), 1)
+    meta = jnp.zeros((1, PATCH), F32)
+    for j in range(n_slots):
+        inside = lax.rem(source_ref[j], GPD).astype(F32)
+        meta = jnp.where(lane == feeder(j), inside, meta)
+    meta_ref[...] = meta
+    loads["w"].wait()
+
+    def pack(i, carry):
+        c1, y1, z1 = i // (Y * Z), (i // Z) % Y, i % Z
+        natural = (z1 * Y + y1) * 2 + c1
+        slot, live = jnp.int32(0), jnp.int32(0)
+        for j in range(n_slots):
+            hit = feeder(j) == natural
+            slot = jnp.where(hit, j, slot)
+            live = jnp.where(hit, 1, live)
+        block = w_ref[slot, xp, :]
+        slots[i] = (block.astype(F32) * live.astype(F32)).astype(BF16)
+        return carry
+
+    lax.fori_loop(0, NP, pack, 0)
     loads["cot"].wait()
-    pl.semaphore_wait(barrier, NP - 1 + X - 1)
-
+    loads["second"].wait()
     own_cot = pltpu.make_async_copy(cot_ref.at[xp, :], cotb.at[c, y, z, :, xf], loc.at[0])
     own_cot.start()
+    own_second = pltpu.make_async_copy(second_ref, second.at[:, xf], loc.at[1])
+    own_second.start()
     own_meta = pltpu.make_async_copy(meta_ref, metab.at[c, y, z], loc.at[2])
     own_meta.start()
+    here = (c * Y + y) * Z + z
+    own_slot = pltpu.make_async_copy(slots.at[here], V.at[here], loc.at[3])
+    own_slot.start()
+    pl.semaphore_wait(barrier, NP - 1 + X - 1)
+
     for k in range(1, X):
         to = step(x, k, X)
         rows = pl.ds(pl.multiple_of(to * PX, PX), PX)
         send(cot_ref.at[rows, :], cotb.at[c, y, z, :, xf], cx_s.at[k - 1], cx_r.at[k - 1], mp=to)
-    loads["second"].wait()
-    own_second = pltpu.make_async_copy(second_ref, second.at[:, xf], loc.at[1])
-    own_second.start()
     for k in range(1, X):
         to = step(x, k, X)
         send(second_ref, second.at[:, xf], sec_s.at[k - 1], sec_r.at[k - 1], mp=to)
-
-    def pack(i, carry):
-        c1, y1, z1 = i // (Y * Z), (i // Z) % Y, i % Z
-        natural = (z1 * Y + y1) * 2 + c1
-        block = w_ref[tab_ref[0, natural], xp, :]
-        live = tab_ref[1, natural]
-        slots[i] = (block.astype(F32) * live.astype(F32)).astype(BF16)
-        return carry
-
-    loads["w"].wait()
-    lax.fori_loop(0, NP, pack, 0)
-
-    own_cot.wait()
-    own_meta.wait()
-    for k in range(1, X):
-        arrive(cotb.at[c, y, z, :, xf], cx_r.at[k - 1])
-    for k in range(1, Z):
-        to = step(z, k, Z)
-        send(cotb.at[c, y, z], cotb.at[c, y, z], cz_s.at[0, k - 1], cz_r.at[0, k - 1], patch_0=to)
-        send(metab.at[c, y, z], metab.at[c, y, z], cz_s.at[1, k - 1], cz_r.at[1, k - 1], patch_0=to)
-
-    here = (c * Y + y) * Z + z
-    own_slot = pltpu.make_async_copy(slots.at[here], V.at[here], loc.at[3])
-    own_slot.start()
 
     def send_slot(j, carry):
         dz, dy, dc = j // (Y * 2), (j // 2) % Y, j % 2
@@ -229,79 +244,127 @@
             src_ref=slots.at[(c1 * Y + y1) * Z + z1],
             dst_ref=V.at[here],
             send_sem=w_s,
-            recv_sem=w_r,
+            recv_sem=w_r.at[c * Y + y],
             device_id={"patch_0": z1, "patch_1": y1, "patch_2": c1, "mp": x},
             device_id_type=pl.DeviceIdType.MESH,
         ).start()
         return carry
 
-    lax.fori_loop(1, NP, send_slot, 0)
-
-    TR = PATCH
-    loads["grid"].wait()
-    loads["first"].wait()
-
-    def first_layer(i, carry):
-        rows = pl.ds(pl.multiple_of(i * TR, TR), TR)
+    def send_slots(dz):
+        lax.fori_loop(max(1, dz * Y * 2), (dz + 1) * Y * 2, send_slot, 0)
+
+    TR = 2 * PATCH
+    T = R // TR
+
+    def first_layer(i):
+        rows = pl.ds(i * TR, TR)
         pre = dot(grid_ref[rows, :], first_ref[...])
         s = jax.nn.sigmoid(pre)
         hidden[rows, :] = (pre * s).astype(BF16)
         slope[rows, :] = s * (1.0 + pre * (1.0 - s))
-        return carry
-
-    lax.fori_loop(0, R // TR, first_layer, 0)
-
+
+    def second_layer(i):
+        rows = pl.ds(i * TR, TR)
+        msg[rows, :] = dot(hidden[rows, :], second[...]).astype(BF16)
+
+    up, down, across = step(y, 1, Y), step(y, Y - 1, Y), step(y, 2, Y)
+    above, below = step(z, 1, Z), step(z, Z - 1, Z)
+    HALVES = (pl.ds(0, PX // 2), pl.ds(PX // 2, PX // 2))
+    y_ways = ((0, up), (1, down)) if Y > 2 else ((0, up),)
+
+    def over_y(k):
+        at = step(z, k % Z, Z)
+        for way, to in y_ways:
+            send(
+                cotb.at[c, y, at],
+                cotb.at[c, y, at],
+                cy_s.at[way, k % Z],
+                cy_r.at[way, k % Z],
+                patch_1=to,
+            )
+
+    def across_y(k):
+        at = step(z, k % Z, Z)
+        for way, frm in ((0, down), (1, up))[: len(y_ways)]:
+            arrive(cotb.at[c, frm, at], cy_r.at[way, k % Z])
+        if Y > 2:
+            for way, frm, to in ((0, down, up), (1, up, down)):
+                send(
+                    cotb.at[c, frm, at, HALVES[way]],
+                    cotb.at[c, frm, at, HALVES[way]],
+                    ch_s.at[way, k % Z],
+                    ch_r.at[way, k % Z],
+                    patch_1=to,
+                )
+
+    def round_z(t):
+        last = 2 * t == Z
+        for way, k, to in ((0, 1 - t, above), (1, t - 1, below)):
+            at = step(z, k % Z, Z)
+            part = cotb.at[c, y, at, HALVES[way]] if last else cotb.at[c, y, at]
+            send(part, part, cz_s.at[way, t - 1], cz_r.at[way, t - 1], patch_0=to)
+
+    def from_z(t):
+        last = 2 * t == Z
+        for way in (0, 1):
+            at = step(z, Z - t, Z) if way == 0 else step(z, t % Z, Z)
+            part = cotb.at[c, y, at, HALVES[way]] if last else cotb.at[c, y, at]
+            arrive(part, cz_r.at[way, t - 1])
+        over_y(Z - t)
+        if not last:
+            over_y(t)
+
+    send_slots(0)
+    own_cot.wait()
+    own_meta.wait()
+    for k in range(1, X):
+        frm = step(x, X - k, X)
+        arrive(cotb.at[c, y, z, :, pl.ds(pl.multiple_of(frm * F, F), F)], cx_r.at[k - 1])
+    round_z(1)
+    over_y(0)
     for k in range(1, Z):
-        frm = step(z, Z - k, Z)
-        arrive(cotb.at[c, y, frm], cz_r.at[0, k - 1])
-        arrive(metab.at[c, y, frm], cz_r.at[1, k - 1])
-    ring = Y == 4
-    up, down, across = step(y, 1, Y), step(y, Y - 1, Y), step(y, 2, Y)
+        to = step(z, k, Z)
+        send(metab.at[c, y, z], metab.at[c, y, z], mz_s.at[k - 1], mz_r.at[k - 1], patch_0=to)
+    steps = Z // 2
+    for t in range(1, steps + 1):
+        for dz in (t, Z - t) if 2 * t < Z else (t,):
+            send_slots(dz)
+        if t == 1:
+            loads["grid"].wait()
+            loads["first"].wait()
+        if t <= T:
+            first_layer(t - 1)
+        from_z(t)
+        if t < steps:
+            round_z(t + 1)
+    for i in range(steps, T):
+        first_layer(i)
+    for k in range(1, Z):
+        arrive(metab.at[c, y, step(z, Z - k, Z)], mz_r.at[k - 1])
     for k in range(1, Y):
         to = step(y, k, Y)
-        send(metab.at[c, y], metab.at[c, y], cy_s.at[1, k - 1], cy_r.at[1, k - 1], patch_1=to)
-        if not ring or k != 2:
-            send(cotb.at[c, y], cotb.at[c, y], cy_s.at[0, k - 1], cy_r.at[0, k - 1], patch_1=to)
-
+        send(metab.at[c, y], metab.at[c, y], my_s.at[k - 1], my_r.at[k - 1], patch_1=to)
+    send(cotb.at[c, y], cotb.at[c, y], cc_s.at[0], cc_r.at[0], patch_2=oc)
     own_second.wait()
     for k in range(1, X):
         frm = step(x, X - k, X)
         arrive(second.at[:, pl.ds(pl.multiple_of(frm * F, F), F)], sec_r.at[k - 1])
-
-    def second_layer(i, carry):
-        rows = pl.ds(pl.multiple_of(i * TR, TR), TR)
-        msg[rows, :] = dot(hidden[rows, :], second[...]).astype(BF16)
-        return carry
-
-    lax.fori_loop(0, R // TR, second_layer, 0)
-
+    order = [0]
+    for t in range(1, steps + 1):
+        order += [Z - t, t] if 2 * t < Z else [t]
+    per = -(-Z // T)
+    for i in range(T):
+        second_layer(i)
+        for k in order[i * per : (i + 1) * per]:
+            across_y(k)
+    for way, frm in ((0, down), (1, up))[: len(y_ways)]:
+        send(cotb.at[c, frm], cotb.at[c, frm], cc_s.at[1 + way], cc_r.at[1 + way], patch_2=oc)
     for k in range(1, Y):
-        frm = step(y, Y - k, Y)
-        arrive(metab.at[c, frm], cy_r.at[1, k - 1])
-        if not ring or k != 2:
-            arrive(cotb.at[c, frm], cy_r.at[0, k - 1])
-    if ring:
-        for i, (frm, to) in enumerate(((down, up), (up, down))):
-            half = pl.ds(i * (Z // 2), Z // 2)
-            send(
-                cotb.at[c, frm, half],
-                cotb.at[c, frm, half],
-                cy_s.at[i, Y - 1],
-                cy_r.at[i, Y - 1],
-                patch_1=to,
-            )
-    send(metab.at[c], metab.at[c], cc_s.at[1], cc_r.at[1], patch_2=oc)
-    arrive(metab.at[oc], cc_r.at[1])
+        arrive(metab.at[c, step(y, Y - k, Y)], my_r.at[k - 1])
+    send(metab.at[c], metab.at[c], mc_s.at[0], mc_r.at[0], patch_2=oc)
+    arrive(metab.at[oc], mc_r.at[0])
 
     own_slot.wait()
-    pltpu.make_async_remote_copy(
-        src_ref=all_but_one(slots, NP),
-        dst_ref=all_but_one(V, NP),
-        send_sem=w_s,
-        recv_sem=w_r,
-        device_id={"patch_0": z, "patch_1": y, "patch_2": oc, "mp": x},
-        device_id_type=pl.DeviceIdType.MESH,
-    ).wait_recv()
     own_natural = (z * Y + y) * 2 + c
     lanes = lax.broadcasted_iota(jnp.int32, (Z, PATCH), 1)
     TC = Z * PX
@@ -325,6 +388,10 @@
             ).astype(BF16)
         return carry
 
+    own_g = c * Y + y
+    arrive(V.at[pl.ds(0, Z - 1)], w_r.at[own_g])
+    for k in range(1, C * Y):
+        arrive(V.at[pl.ds(0, Z)], w_r.at[lax.rem(own_g + k, C * Y)])
     lax.fori_loop(0, C * Y, spread, 0)
 
 
@@ -336,10 +403,11 @@
         yy = step(y, k % Y, Y)
         c_send[yy] = contribution(oc, yy).astype(BF16).reshape(Z, PX, D)
         send(c_send.at[yy], c_recv.at[yy], fc_s.at[k - 1], fc_r.at[k - 1], patch_2=oc)
-    if ring:
-        for i in range(2):
-            arrive(cotb.at[c, across, pl.ds(i * (Z // 2), Z // 2)], cy_r.at[i, Y - 1])
-    send(cotb.at[c], cotb.at[c], cc_s.at[0], cc_r.at[0], patch_2=oc)
+    if Y > 2:
+        for k in order:
+            for way in (0, 1):
+                arrive(cotb.at[c, across, step(z, k % Z, Z), HALVES[way]], ch_r.at[way, k % Z])
+        send(cotb.at[c, across], cotb.at[c, across], cc_s.at[3], cc_r.at[3], patch_2=oc)
     for k in range(1, Y + 1):
         yy = step(y, k % Y, Y)
         part = contribution(c, yy)
@@ -351,14 +419,16 @@
         else:
             y_own[...] = part.reshape(Z, PX, D)
 
-    arrive(cotb.at[oc], cc_r.at[0])
+    columns = (y, down, up, across) if Y > 2 else (y, up)
+    for i, yy in enumerate(columns):
+        arrive(cotb.at[oc, yy], cc_r.at[i])
 
     def message_gradient(i, carry):
         rows = pl.ds(pl.multiple_of(i * TR, TR), TR)
         gm[rows, :] = dot(vbig_t[rows, :], cotb[...].reshape(NP * PX, D)).astype(BF16)
         return carry
 
-    lax.fori_loop(0, GPD, message_gradient, 0)
+    lax.fori_loop(0, R // TR, message_gradient, 0)
 
     def halves(which, left_ref, right_ref):
         for core in (oc, c):
@@ -481,7 +551,7 @@
         src_ref=all_but_one(slots, NP),
         dst_ref=all_but_one(V, NP),
         send_sem=w_s,
-        recv_sem=w_r,
+        recv_sem=w_r.at[0],
         device_id={"patch_0": z, "patch_1": y, "patch_2": oc, "mp": x},
         device_id_type=pl.DeviceIdType.MESH,
     ).wait_send()
@@ -513,16 +583,12 @@
     GPD = R // PATCH
     HC = D // 2
     ZR = HC // Z
-    slots_of = edge_weight.shape[0]
-    hit = (block_source // GPD)[:, None] == jnp.arange(PATCH)[None, :]
-    values = jnp.stack([jnp.arange(slots_of, dtype=jnp.int32), block_live, block_source % GPD])
-    tab = jnp.sum(jnp.where(hit[None], values[:, :, None], 0), axis=1)
-    meta = tab[2:3].astype(F32)
     scaling = 1.0 / math.sqrt(R * NP)
 
     vm = pltpu.VMEM
     dma = pltpu.SemaphoreType.DMA
     scratch = [
+        vm((1, PATCH), F32),
         vm(grid_latent.shape, BF16),
         vm(mesh_latent.shape, BF16),
         vm(edge_weight.shape, BF16),
@@ -561,17 +627,25 @@
         vm((2, ZR, F), BF16),
         vm((C, Z, 2, ZR, F), BF16),
         dma,
-        dma,
+        dma((C * Y,)),
         dma((X - 1,)),
         dma((X - 1,)),
         dma((X - 1,)),
         dma((X - 1,)),
-        dma((2, Z - 1)),
-        dma((2, Z - 1)),
-        dma((2, Y)),
-        dma((2, Y)),
-        dma((2,)),
-        dma((2,)),
+        dma((2, Z // 2)),
+        dma((2, Z // 2)),
+        dma((2, Z)),
+        dma((2, Z)),
+        dma((2, Z)),
+        dma((2, Z)),
+        dma((4,)),
+        dma((4,)),
+        dma((Z - 1,)),
+        dma((Z - 1,)),
+        dma((Y - 1,)),
+        dma((Y - 1,)),
+        dma((1,)),
+        dma((1,)),
         dma((Y,)),
         dma((Y,)),
         dma((Y - 1,)),
@@ -603,7 +677,7 @@
             jax.ShapeDtypeStruct((D, F), F32),
             jax.ShapeDtypeStruct((H, F), F32),
         ),
-        in_specs=[pl.BlockSpec(memory_space=pltpu.SMEM), in_vmem]
+        in_specs=[pl.BlockSpec(memory_space=pltpu.SMEM)] * 2
         + [pl.BlockSpec(memory_space=pl.ANY)] * 6,
         out_specs=(in_vmem, in_vmem, in_vmem),
         scratch_shapes=scratch,
@@ -611,8 +685,8 @@
             collective_id=0, has_side_effects=True, vmem_limit_bytes=62 * 1024 * 1024
         ),
     )(
-        tab,
-        meta,
+        block_source,
+        block_live,
         grid_latent,
         mesh_latent,
         edge_weight,
@@ -623,12 +697,12 @@
     return mesh_out, grad_first, grad_second
 
 
+def torus_of(mesh):
+    return Mesh(mesh.devices.reshape(8, 4, 2, mesh.shape["mp"]), AXES)
+
+
 def solution(mesh):
-    mp = mesh.shape["mp"]
-    cores = 2
-    rows = mesh.shape["patch"] // cores
-    depth = 8 if rows % 8 == 0 else 2
-    torus = Mesh(mesh.devices.reshape(depth, rows // depth, cores, mp), AXES)
+    torus = torus_of(mesh)
     in_specs = (
         P(PATCH_AXES, None),
         P(PATCH_AXES, "mp"),

time: 89.6 us -> 89.2 us (level)
  Pallas kernels: 83 us -> 84.6 us
  local copies, waits for them, and re-layouts: 5.07 us -> 3.79 us
    pallas_call x1, Pallas kernels: 83 us -> 84.6 us  [per_device(): pl.pallas_call(functools.partial(kernel, (Z, Y, C, X), scaling), out_shap...]
    unnamed x11 -> x5, local copies, waits for them, and re-layouts: 5.07 us -> 3.79 us
where the time goes in v3:
time: 89.2 us; the launch traced here: 89.1 us
  Pallas kernels  84.6 us (95%)
  local copies, waits for them, and re-layouts  3.79 us (4%)
    pallas_call x1, Pallas kernels, per_device(): pl.pallas_call(functools.partial(kernel, (Z, Y, C, X), scaling), out_shap...  84.6 us
    unnamed x5, local copies, waits for them, and re-layouts  3.79 us

profile of v3, /device:TPU:1, one launch (start us, length us, event | category | flops | bytes accessed | tf_op | source)
XLA Modules:
  0.0 89.1 jit_solution(1781443598997530761)
XLA Ops:
  0.6 84.6 %shard_map.103 = (bf16[128,128]{1,0:T(8,128)(2,1)}, f32[512,128]{1,0:T(8,128)}, f32[512,128]{1,0:T(8,128)}) custom-call(s32[12]{0:T(128)} %source_ref.1, s32[12]{0:T(128)} %live_ref.1, bf16[1024,512]{1,0:T(8,128)(2,1)} %grid_in.1, bf16[128,128]{1,0:T(8,128)(2,1)} %latent_in.1, bf16[12,128,128]{2,1,0:T(8,128)(2,1)} %w_in.1, bf16[512,512]{1,0:T(8,128)(2,1)} %first_in.1, ...), custom_call_target="tpu_custom_call" | custom-call | tf_op jit(solution)/shard_map/pallas_call | solution.py:673
  85.3 1.4 %copy.14 = bf16[128,128]{1,0:T(8,128)(2,1)} copy(bf16[128,128]{1,0:T(8,128)(2,1)} %get-tuple-element.6) | data formatting | bytes 65536
  86.6 0.0 copy-start
  86.6 1.7 %copy.15 = f32[512,128]{1,0:T(8,128)} copy(f32[512,128]{1,0:T(8,128)} %get-tuple-element.7) | data formatting | bytes 524288
  88.4 0.0 copy-done
  88.4 0.7 copy.16
Async XLA Ops:
  86.6 1.7 %copy-start = (f32[512,128]{1,0:T(8,128)S(1)}, f32[512,128]{1,0:T(8,128)}, u32[]{:S(2)}) copy-start(f32[512,128]{1,0:T(8,128)} %get-tuple-element.8) | copy-start | bytes 786436

commit v4 on v3

--- a/solution.py
+++ b/solution.py
@@ -82,8 +82,6 @@
     cz_r,
     cy_s,
     cy_r,
-    ch_s,
-    ch_r,
     cc_s,
     cc_r,
     mz_s,
@@ -181,14 +179,22 @@
         )
         return carry
 
-    for k in range(1, X):
+    def greet_mp(j, carry):
         pl.semaphore_signal(
             barrier,
             inc=1,
-            device_id={"patch_0": z, "patch_1": y, "patch_2": c, "mp": step(x, k, X)},
+            device_id={
+                "patch_0": lax.rem(z + j % Z, Z),
+                "patch_1": y,
+                "patch_2": c,
+                "mp": lax.rem(x + j // Z, X),
+            },
             device_id_type=pl.DeviceIdType.MESH,
         )
+        return carry
+
     lax.fori_loop(1, NP, greet, 0)
+    lax.fori_loop(Z, X * Z, greet_mp, 0)
 
     n_slots = w_in.shape[0]
 
@@ -227,12 +233,33 @@
     here = (c * Y + y) * Z + z
     own_slot = pltpu.make_async_copy(slots.at[here], V.at[here], loc.at[3])
     own_slot.start()
-    pl.semaphore_wait(barrier, NP - 1 + X - 1)
-
-    for k in range(1, X):
-        to = step(x, k, X)
-        rows = pl.ds(pl.multiple_of(to * PX, PX), PX)
-        send(cot_ref.at[rows, :], cotb.at[c, y, z, :, xf], cx_s.at[k - 1], cx_r.at[k - 1], mp=to)
+    pl.semaphore_wait(barrier, NP - 1 + (X - 1) * Z)
+
+    own_meta.wait()
+    near = [0]
+    for t in range(1, Z // 2 + 1):
+        near += [t, Z - t] if 2 * t < Z else [t]
+    for k in near:
+        for m in range(X):
+            if k or m:
+                to = step(x, m, X)
+                rows = pl.ds(pl.multiple_of(to * PX, PX), PX)
+                send(
+                    cot_ref.at[rows, :],
+                    cotb.at[c, y, z, :, xf],
+                    cz_s.at[k, m],
+                    cz_r.at[k],
+                    patch_0=step(z, k, Z),
+                    mp=to,
+                )
+        if k:
+            send(
+                metab.at[c, y, z],
+                metab.at[c, y, z],
+                mz_s.at[k - 1],
+                mz_r.at[k - 1],
+                patch_0=step(z, k, Z),
+            )
     for k in range(1, X):
         to = step(x, k, X)
         send(second_ref, second.at[:, xf], sec_s.at[k - 1], sec_r.at[k - 1], mp=to)
@@ -250,8 +277,7 @@
         ).start()
         return carry
 
-    def send_slots(dz):
-        lax.fori_loop(max(1, dz * Y * 2), (dz + 1) * Y * 2, send_slot, 0)
+    lax.fori_loop(1, NP, send_slot, 0)
 
     TR = 2 * PATCH
     T = R // TR
@@ -267,101 +293,43 @@
         rows = pl.ds(i * TR, TR)
         msg[rows, :] = dot(hidden[rows, :], second[...]).astype(BF16)
 
-    up, down, across = step(y, 1, Y), step(y, Y - 1, Y), step(y, 2, Y)
-    above, below = step(z, 1, Z), step(z, Z - 1, Z)
-    HALVES = (pl.ds(0, PX // 2), pl.ds(PX // 2, PX // 2))
-    y_ways = ((0, up), (1, down)) if Y > 2 else ((0, up),)
-
     def over_y(k):
-        at = step(z, k % Z, Z)
-        for way, to in y_ways:
-            send(
-                cotb.at[c, y, at],
-                cotb.at[c, y, at],
-                cy_s.at[way, k % Z],
-                cy_r.at[way, k % Z],
-                patch_1=to,
-            )
-
-    def across_y(k):
-        at = step(z, k % Z, Z)
-        for way, frm in ((0, down), (1, up))[: len(y_ways)]:
-            arrive(cotb.at[c, frm, at], cy_r.at[way, k % Z])
-        if Y > 2:
-            for way, frm, to in ((0, down, up), (1, up, down)):
-                send(
-                    cotb.at[c, frm, at, HALVES[way]],
-                    cotb.at[c, frm, at, HALVES[way]],
-                    ch_s.at[way, k % Z],
-                    ch_r.at[way, k % Z],
-                    patch_1=to,
-                )
-
-    def round_z(t):
-        last = 2 * t == Z
-        for way, k, to in ((0, 1 - t, above), (1, t - 1, below)):
-            at = step(z, k % Z, Z)
-            part = cotb.at[c, y, at, HALVES[way]] if last else cotb.at[c, y, at]
-            send(part, part, cz_s.at[way, t - 1], cz_r.at[way, t - 1], patch_0=to)
-
-    def from_z(t):
-        last = 2 * t == Z
-        for way in (0, 1):
-            at = step(z, Z - t, Z) if way == 0 else step(z, t % Z, Z)
-            part = cotb.at[c, y, at, HALVES[way]] if last else cotb.at[c, y, at]
-            arrive(part, cz_r.at[way, t - 1])
-        over_y(Z - t)
-        if not last:
-            over_y(t)
-
-    send_slots(0)
-    own_cot.wait()
-    own_meta.wait()
-    for k in range(1, X):
-        frm = step(x, X - k, X)
-        arrive(cotb.at[c, y, z, :, pl.ds(pl.multiple_of(frm * F, F), F)], cx_r.at[k - 1])
-    round_z(1)
-    over_y(0)
-    for k in range(1, Z):
-        to = step(z, k, Z)
-        send(metab.at[c, y, z], metab.at[c, y, z], mz_s.at[k - 1], mz_r.at[k - 1], patch_0=to)
-    steps = Z // 2
-    for t in range(1, steps + 1):
-        for dz in (t, Z - t) if 2 * t < Z else (t,):
-            send_slots(dz)
-        if t == 1:
-            loads["grid"].wait()
-            loads["first"].wait()
-        if t <= T:
-            first_layer(t - 1)
-        from_z(t)
-        if t < steps:
-            round_z(t + 1)
-    for i in range(steps, T):
+        at = step(z, (Z - k) % Z, Z)
+        if k:
+            arrive(cotb.at[c, y, at], cz_r.at[k])
+        else:
+            own_cot.wait()
+            arrive(cotb.at[c, y, at, :, pl.ds(0, (X - 1) * F)], cz_r.at[k])
+        for m in range(1, Y):
+            block = cotb.at[c, y, at]
+            send(block, block, cy_s.at[m - 1, k], cy_r.at[m - 1], patch_1=step(y, m, Y))
+
+    loads["grid"].wait()
+    loads["first"].wait()
+    per = -(-Z // T)
+    for i in range(T):
         first_layer(i)
+        for k in near[i * per : (i + 1) * per]:
+            over_y(k)
     for k in range(1, Z):
         arrive(metab.at[c, y, step(z, Z - k, Z)], mz_r.at[k - 1])
-    for k in range(1, Y):
-        to = step(y, k, Y)
-        send(metab.at[c, y], metab.at[c, y], my_s.at[k - 1], my_r.at[k - 1], patch_1=to)
+    for m in range(1, Y):
+        to = step(y, m, Y)
+        send(metab.at[c, y], metab.at[c, y], my_s.at[m - 1], my_r.at[m - 1], patch_1=to)
     send(cotb.at[c, y], cotb.at[c, y], cc_s.at[0], cc_r.at[0], patch_2=oc)
     own_second.wait()
     for k in range(1, X):
         frm = step(x, X - k, X)
         arrive(second.at[:, pl.ds(pl.multiple_of(frm * F, F), F)], sec_r.at[k - 1])
-    order = [0]
-    for t in range(1, steps + 1):
-        order += [Z - t, t] if 2 * t < Z else [t]
-    per = -(-Z // T)
     for i in range(T):
         second_layer(i)
-        for k in order[i * per : (i + 1) * per]:
-            across_y(k)
-    for way, frm in ((0, down), (1, up))[: len(y_ways)]:
-        send(cotb.at[c, frm], cotb.at[c, frm], cc_s.at[1 + way], cc_r.at[1 + way], patch_2=oc)
-    for k in range(1, Y):
-        arrive(metab.at[c, step(y, Y - k, Y)], my_r.at[k - 1])
+    for m in range(1, Y):
+        arrive(metab.at[c, step(y, Y - m, Y)], my_r.at[m - 1])
     send(metab.at[c], metab.at[c], mc_s.at[0], mc_r.at[0], patch_2=oc)
+    for m in range(1, Y):
+        frm = step(y, Y - m, Y)
+        arrive(cotb.at[c, frm], cy_r.at[m - 1])
+        send(cotb.at[c, frm], cotb.at[c, frm], cc_s.at[m], cc_r.at[m], patch_2=oc)
     arrive(metab.at[oc], mc_r.at[0])
 
     own_slot.wait()
@@ -403,11 +371,6 @@
         yy = step(y, k % Y, Y)
         c_send[yy] = contribution(oc, yy).astype(BF16).reshape(Z, PX, D)
         send(c_send.at[yy], c_recv.at[yy], fc_s.at[k - 1], fc_r.at[k - 1], patch_2=oc)
-    if Y > 2:
-        for k in order:
-            for way in (0, 1):
-                arrive(cotb.at[c, across, step(z, k % Z, Z), HALVES[way]], ch_r.at[way, k % Z])
-        send(cotb.at[c, across], cotb.at[c, across], cc_s.at[3], cc_r.at[3], patch_2=oc)
     for k in range(1, Y + 1):
         yy = step(y, k % Y, Y)
         part = contribution(c, yy)
@@ -419,9 +382,8 @@
         else:
             y_own[...] = part.reshape(Z, PX, D)
 
-    columns = (y, down, up, across) if Y > 2 else (y, up)
-    for i, yy in enumerate(columns):
-        arrive(cotb.at[oc, yy], cc_r.at[i])
+    for m in range(Y):
+        arrive(cotb.at[oc, step(y, Y - m, Y)], cc_r.at[m])
 
     def message_gradient(i, carry):
         rows = pl.ds(pl.multiple_of(i * TR, TR), TR)
@@ -632,12 +594,10 @@
         dma((X - 1,)),
         dma((X - 1,)),
         dma((X - 1,)),
-        dma((2, Z // 2)),
-        dma((2, Z // 2)),
-        dma((2, Z)),
-        dma((2, Z)),
-        dma((2, Z)),
-        dma((2, Z)),
+        dma((Z, X)),
+        dma((Z,)),
+        dma((Y - 1, Z)),
+        dma((Y - 1,)),
         dma((4,)),
         dma((4,)),
         dma((Z - 1,)),

time: 89.2 us -> 87.1 us (0.976)
  Pallas kernels: 84.6 us -> 82.4 us
    pallas_call x1, Pallas kernels: 84.6 us -> 82.4 us  [per_device(): pl.pallas_call(functools.partial(kernel, (Z, Y, C, X), scaling), out_shap...]
where the time goes in v4:
time: 87.1 us; the launch traced here: 86.9 us
  Pallas kernels  82.4 us (95%)
  local copies, waits for them, and re-layouts  3.79 us (4%)
    pallas_call x1, Pallas kernels, per_device(): pl.pallas_call(functools.partial(kernel, (Z, Y, C, X), scaling), out_shap...  82.4 us
    unnamed x5, local copies, waits for them, and re-layouts  3.79 us

profile of v4, /device:TPU:1, one launch (start us, length us, event | category | flops | bytes accessed | tf_op | source)
XLA Modules:
  0.0 86.9 jit_solution(15824163520912778075)
XLA Ops:
  0.6 82.4 %shard_map.103 = (bf16[128,128]{1,0:T(8,128)(2,1)}, f32[512,128]{1,0:T(8,128)}, f32[512,128]{1,0:T(8,128)}) custom-call(s32[12]{0:T(128)} %source_ref.1, s32[12]{0:T(128)} %live_ref.1, bf16[1024,512]{1,0:T(8,128)(2,1)} %grid_in.1, bf16[128,128]{1,0:T(8,128)(2,1)} %latent_in.1, bf16[12,128,128]{2,1,0:T(8,128)(2,1)} %w_in.1, bf16[512,512]{1,0:T(8,128)(2,1)} %first_in.1, ...), custom_call_target="tpu_custom_call" | custom-call | tf_op jit(solution)/shard_map/pallas_call | solution.py:633
  83.1 1.4 %copy.14 = bf16[128,128]{1,0:T(8,128)(2,1)} copy(bf16[128,128]{1,0:T(8,128)(2,1)} %get-tuple-element.6) | data formatting | bytes 65536
  84.5 0.0 copy-start
  84.5 1.7 %copy.15 = f32[512,128]{1,0:T(8,128)} copy(f32[512,128]{1,0:T(8,128)} %get-tuple-element.7) | data formatting | bytes 524288
  86.2 0.0 copy-done
  86.2 0.7 copy.16
Async XLA Ops:
  84.5 1.7 %copy-start = (f32[512,128]{1,0:T(8,128)S(1)}, f32[512,128]{1,0:T(8,128)}, u32[]{:S(2)}) copy-start(f32[512,128]{1,0:T(8,128)} %get-tuple-element.8) | copy-start | bytes 786436

commit v5 on v4

--- a/solution.py
+++ b/solution.py
@@ -32,8 +32,7 @@
     second_in,
     cot_in,
     mesh_out,
-    first_out,
-    second_out,
+    fin,
     meta_ref,
     grid_ref,
     latent_ref,
@@ -71,7 +70,6 @@
     gz_recv,
     gy,
     own,
-    fin,
     w_s,
     w_r,
     sec_s,
@@ -210,7 +208,7 @@
     loads["w"].wait()
 
     def pack(i, carry):
-        c1, y1, z1 = i // (Y * Z), (i // Z) % Y, i % Z
+        z1, c1, y1 = i // (2 * Y), (i // Y) % 2, i % Y
         natural = (z1 * Y + y1) * 2 + c1
         slot, live = jnp.int32(0), jnp.int32(0)
         for j in range(n_slots):
@@ -224,13 +222,13 @@
     lax.fori_loop(0, NP, pack, 0)
     loads["cot"].wait()
     loads["second"].wait()
-    own_cot = pltpu.make_async_copy(cot_ref.at[xp, :], cotb.at[c, y, z, :, xf], loc.at[0])
+    own_cot = pltpu.make_async_copy(cot_ref.at[xp, :], cotb.at[z, c, y, :, xf], loc.at[0])
     own_cot.start()
     own_second = pltpu.make_async_copy(second_ref, second.at[:, xf], loc.at[1])
     own_second.start()
-    own_meta = pltpu.make_async_copy(meta_ref, metab.at[c, y, z], loc.at[2])
+    own_meta = pltpu.make_async_copy(meta_ref, metab.at[z, c, y], loc.at[2])
     own_meta.start()
-    here = (c * Y + y) * Z + z
+    here = (z * 2 + c) * Y + y
     own_slot = pltpu.make_async_copy(slots.at[here], V.at[here], loc.at[3])
     own_slot.start()
     pl.semaphore_wait(barrier, NP - 1 + (X - 1) * Z)
@@ -246,7 +244,7 @@
                 rows = pl.ds(pl.multiple_of(to * PX, PX), PX)
                 send(
                     cot_ref.at[rows, :],
-                    cotb.at[c, y, z, :, xf],
+                    cotb.at[z, c, y, :, xf],
                     cz_s.at[k, m],
                     cz_r.at[k],
                     patch_0=step(z, k, Z),
@@ -254,8 +252,8 @@
                 )
         if k:
             send(
-                metab.at[c, y, z],
-                metab.at[c, y, z],
+                metab.at[z, c, y],
+                metab.at[z, c, y],
                 mz_s.at[k - 1],
                 mz_r.at[k - 1],
                 patch_0=step(z, k, Z),
@@ -268,10 +266,10 @@
         dz, dy, dc = j // (Y * 2), (j // 2) % Y, j % 2
         z1, y1, c1 = lax.rem(z + dz, Z), lax.rem(y + dy, Y), lax.rem(c + dc, 2)
         pltpu.make_async_remote_copy(
-            src_ref=slots.at[(c1 * Y + y1) * Z + z1],
+            src_ref=slots.at[(z1 * 2 + c1) * Y + y1],
             dst_ref=V.at[here],
             send_sem=w_s,
-            recv_sem=w_r.at[c * Y + y],
+            recv_sem=w_r.at[z],
             device_id={"patch_0": z1, "patch_1": y1, "patch_2": c1, "mp": x},
             device_id_type=pl.DeviceIdType.MESH,
         ).start()
@@ -296,12 +294,12 @@
     def over_y(k):
         at = step(z, (Z - k) % Z, Z)
         if k:
-            arrive(cotb.at[c, y, at], cz_r.at[k])
+            arrive(cotb.at[at, c, y], cz_r.at[k])
         else:
             own_cot.wait()
-            arrive(cotb.at[c, y, at, :, pl.ds(0, (X - 1) * F)], cz_r.at[k])
+            arrive(cotb.at[at, c, y, :, pl.ds(0, (X - 1) * F)], cz_r.at[k])
         for m in range(1, Y):
-            block = cotb.at[c, y, at]
+            block = cotb.at[at, c, y]
             send(block, block, cy_s.at[m - 1, k], cy_r.at[m - 1], patch_1=step(y, m, Y))
 
     loads["grid"].wait()
@@ -312,11 +310,11 @@
         for k in near[i * per : (i + 1) * per]:
             over_y(k)
     for k in range(1, Z):
-        arrive(metab.at[c, y, step(z, Z - k, Z)], mz_r.at[k - 1])
+        arrive(metab.at[step(z, Z - k, Z), c, y], mz_r.at[k - 1])
     for m in range(1, Y):
         to = step(y, m, Y)
-        send(metab.at[c, y], metab.at[c, y], my_s.at[m - 1], my_r.at[m - 1], patch_1=to)
-    send(cotb.at[c, y], cotb.at[c, y], cc_s.at[0], cc_r.at[0], patch_2=oc)
+        send(metab.at[:, c, y], metab.at[:, c, y], my_s.at[m - 1], my_r.at[m - 1], patch_1=to)
+    send(cotb.at[:, c, y], cotb.at[:, c, y], cc_s.at[0], cc_r.at[0], patch_2=oc)
     own_second.wait()
     for k in range(1, X):
         frm = step(x, X - k, X)
@@ -324,48 +322,48 @@
     for i in range(T):
         second_layer(i)
     for m in range(1, Y):
-        arrive(metab.at[c, step(y, Y - m, Y)], my_r.at[m - 1])
-    send(metab.at[c], metab.at[c], mc_s.at[0], mc_r.at[0], patch_2=oc)
+        arrive(metab.at[:, c, step(y, Y - m, Y)], my_r.at[m - 1])
+    send(metab.at[:, c], metab.at[:, c], mc_s.at[0], mc_r.at[0], patch_2=oc)
     for m in range(1, Y):
         frm = step(y, Y - m, Y)
-        arrive(cotb.at[c, frm], cy_r.at[m - 1])
-        send(cotb.at[c, frm], cotb.at[c, frm], cc_s.at[m], cc_r.at[m], patch_2=oc)
-    arrive(metab.at[oc], mc_r.at[0])
-
-    own_slot.wait()
+        arrive(cotb.at[:, c, frm], cy_r.at[m - 1])
+        send(cotb.at[:, c, frm], cotb.at[:, c, frm], cc_s.at[m], cc_r.at[m], patch_2=oc)
+    arrive(metab.at[:, oc], mc_r.at[0])
+
     own_natural = (z * Y + y) * 2 + c
-    lanes = lax.broadcasted_iota(jnp.int32, (Z, PATCH), 1)
+    PL = C * Y
+    TP = PL * PX
     TC = Z * PX
+    lanes = lax.broadcasted_iota(jnp.int32, (PL, PATCH), 1)
 
     def spread(i, carry):
-        meta = metab[i // Y, lax.rem(i, Y)].reshape(Z, PATCH)
+        at = lax.rem(z + i, Z)
+        meta = metab[at].reshape(PL, PATCH)
         patch_of = jnp.sum(jnp.where(lanes == own_natural, meta, 0.0), axis=1, keepdims=True)
         patch_rows = jnp.broadcast_to(
-            jnp.broadcast_to(patch_of, (Z, PATCH))[:, None, :], (Z, PX, PATCH)
-        ).reshape(TC, PATCH)
-        blocks = V[pl.ds(pl.multiple_of(i * Z, Z), Z)].reshape(TC, PATCH).astype(F32)
-        rows = pl.ds(pl.multiple_of(i * TC, TC), TC)
+            jnp.broadcast_to(patch_of, (PL, PATCH))[:, None, :], (PL, PX, PATCH)
+        ).reshape(TP, PATCH)
+        blocks = V[pl.ds(pl.multiple_of(at * PL, PL), PL)].reshape(TP, PATCH).astype(F32)
+        cols = pl.ds(pl.multiple_of(at * TP, TP), TP)
         blocks_t = blocks.T
         patch_cols = patch_rows.T
         for g in range(GPD):
-            vbig[rows, g * PATCH : (g + 1) * PATCH] = jnp.where(
-                patch_rows == float(g), blocks, 0.0
-            ).astype(BF16)
-            vbig_t[g * PATCH : (g + 1) * PATCH, rows] = jnp.where(
+            part = jnp.where(patch_rows == float(g), blocks, 0.0).astype(BF16)
+            vbig[:, at, :, g * PATCH : (g + 1) * PATCH] = part.reshape(PL, PX, PATCH)
+            vbig_t[g * PATCH : (g + 1) * PATCH, cols] = jnp.where(
                 patch_cols == float(g), blocks_t, 0.0
             ).astype(BF16)
         return carry
 
-    own_g = c * Y + y
-    arrive(V.at[pl.ds(0, Z - 1)], w_r.at[own_g])
-    for k in range(1, C * Y):
-        arrive(V.at[pl.ds(0, Z)], w_r.at[lax.rem(own_g + k, C * Y)])
-    lax.fori_loop(0, C * Y, spread, 0)
+    own_slot.wait()
+    for k in near:
+        frm = step(z, (Z - k) % Z, Z)
+        arrive(V.at[pl.ds(0, PL if k else PL - 1)], w_r.at[frm])
+        spread((Z - k) % Z, 0)
 
 
     def contribution(core, yy):
-        at = pl.multiple_of((core * Y + yy) * TC, TC)
-        return dot(vbig[pl.ds(at, TC), :], msg[...])
+        return dot(vbig[core * Y + yy].reshape(TC, R), msg[...])
 
     for k in range(1, Y + 1):
         yy = step(y, k % Y, Y)
@@ -383,7 +381,7 @@
             y_own[...] = part.reshape(Z, PX, D)
 
     for m in range(Y):
-        arrive(cotb.at[oc, step(y, Y - m, Y)], cc_r.at[m])
+        arrive(cotb.at[:, oc, step(y, Y - m, Y)], cc_r.at[m])
 
     def message_gradient(i, carry):
         rows = pl.ds(pl.multiple_of(i * TR, TR), TR)
@@ -438,17 +436,6 @@
 
     halves(1, grid_ref, gpre)
 
-    for k in range(1, Y):
-        arrive(y_recv.at[k - 1], fy_r.at[k - 1])
-    total = y_own[...]
-    for k in range(1, Y):
-        total = total + y_recv[k - 1].astype(F32)
-    y_own[...] = total
-    z_send[...] = total.astype(BF16)
-    for k in range(1, Z):
-        to = step(z, k, Z)
-        send(z_send.at[to], z_recv.at[k - 1], fz_s.at[k - 1], fz_r.at[k - 1], patch_0=to)
-
     over_mp(1)
 
     ZR = HC // Z
@@ -463,6 +450,37 @@
         to = step(z, k, Z)
         send(gz_send.at[to], gz_recv.at[k - 1], gz_s.at[k - 1], gz_r.at[k - 1], patch_0=to)
 
+    for k in range(1, Y):
+        arrive(y_recv.at[k - 1], fy_r.at[k - 1])
+    total = y_own[...]
+    for k in range(1, Y):
+        total = total + y_recv[k - 1].astype(F32)
+    y_own[...] = total
+    z_send[...] = total.astype(BF16)
+    for k in range(1, Z):
+        to = step(z, k, Z)
+        send(z_send.at[to], z_recv.at[k - 1], fz_s.at[k - 1], fz_r.at[k - 1], patch_0=to)
+
+    total = g_own[:, x, pl.ds(pl.multiple_of(z * ZR, ZR), ZR)]
+    for k in range(1, Z):
+        arrive(gz_recv.at[k - 1], gz_r.at[k - 1])
+        total = total + gz_recv[k - 1].astype(F32)
+    gy[y] = total
+    for k in range(1, Y):
+        to = step(y, k, Y)
+        send(gy.at[y], gy.at[y], gy_s.at[k - 1], gy_r.at[k - 1], patch_1=to)
+
+    for k in range(1, Y):
+        arrive(gy.at[step(y, Y - k, Y)], gy_r.at[k - 1])
+    total = gy[0]
+    for yy in range(1, Y):
+        total = total + gy[yy]
+    own[...] = total.astype(BF16)
+    for k in range(1, Z):
+        to = step(z, k, Z)
+        send(own, fin.at[c, z], az_s.at[k - 1], az_r.at[k - 1], patch_0=to)
+    fin[c, z] = own[...]
+
     total = y_own[z]
     for k in range(1, Z):
         arrive(z_recv.at[k - 1], fz_r.at[k - 1])
@@ -475,40 +493,15 @@
         to = step(x, k, X)
         send(x_send.at[to], x_recv.at[x], fx_s.at[k - 1], fx_r.at[k - 1], mp=to)
 
-    total = g_own[:, x, pl.ds(pl.multiple_of(z * ZR, ZR), ZR)]
     for k in range(1, Z):
-        arrive(gz_recv.at[k - 1], gz_r.at[k - 1])
-        total = total + gz_recv[k - 1].astype(F32)
-    gy[y] = total
-    for k in range(1, Y):
-        to = step(y, k, Y)
-        send(gy.at[y], gy.at[y], gy_s.at[k - 1], gy_r.at[k - 1], patch_1=to)
-
+        arrive(fin.at[c, step(z, Z - k, Z)], az_r.at[k - 1])
+    send(fin.at[c], fin.at[c], ac_s.at[0], ac_r.at[0], patch_2=oc)
     own_sum.wait()
     for k in range(1, X):
         arrive(x_recv.at[step(x, X - k, X)], fx_r.at[k - 1])
     loads["latent"].wait()
     mesh_out[...] = (latent_ref[...].astype(F32) + x_recv[...].reshape(PATCH, F)).astype(BF16)
-
-    for k in range(1, Y):
-        arrive(gy.at[step(y, Y - k, Y)], gy_r.at[k - 1])
-    total = gy[0]
-    for yy in range(1, Y):
-        total = total + gy[yy]
-    own[...] = total.astype(BF16)
-    for k in range(1, Z):
-        to = step(z, k, Z)
-        send(own, fin.at[c, z], az_s.at[k - 1], az_r.at[k - 1], patch_0=to)
-    fin[c, z] = own[...]
-    for k in range(1, Z):
-        arrive(fin.at[c, step(z, Z - k, Z)], az_r.at[k - 1])
-    send(fin.at[c], fin.at[c], ac_s.at[0], ac_r.at[0], patch_2=oc)
     arrive(fin.at[oc], ac_r.at[0])
-    for core in range(2):
-        rows = slice(core * HC, (core + 1) * HC)
-        second_out[rows, :] = fin[core, :, 0].reshape(HC, F).astype(F32)
-        first_out[rows, :] = fin[core, :, 1].reshape(HC, F).astype(F32)
-
     pltpu.make_async_remote_copy(
         src_ref=all_but_one(slots, NP),
         dst_ref=all_but_one(V, NP),
@@ -519,6 +512,12 @@
     ).wait_send()
     for src, dst, ss, rs in sent:
         pltpu.make_async_copy(src, src, ss).wait()
+
+
+def hand_out(mesh_sum, sums, mesh_out, first_out, second_out):
+    mesh_out[...] = mesh_sum[...]
+    second_out[...] = sums[:, :, 0].reshape(second_out.shape).astype(F32)
+    first_out[...] = sums[:, :, 1].reshape(first_out.shape).astype(F32)
 
 
 def all_but_one(ref, n):
@@ -559,13 +558,13 @@
         vm(mesh_cotangent.shape, BF16),
         vm((NP, PX, PATCH), BF16),
         vm((NP, PX, PATCH), BF16),
-        vm((C, Y, Z, PX, D), BF16),
-        vm((C, Y, Z, 1, PATCH), F32),
+        vm((Z, C, Y, PX, D), BF16),
+        vm((Z, C, Y, 1, PATCH), F32),
         vm((H, D), BF16),
         vm((R, H), F32),
         vm((R, H), BF16),
         vm((R, D), BF16),
-        vm((NP * PX, R), BF16),
+        vm((C * Y, Z, PX, R), BF16),
         vm((R, NP * PX), BF16),
         vm((Y, Z, PX, D), BF16),
         vm((Y, Z, PX, D), BF16),
@@ -587,9 +586,8 @@
         vm((Z - 1, 2, ZR, F), BF16),
         vm((Y, 2, ZR, F), F32),
         vm((2, ZR, F), BF16),
-        vm((C, Z, 2, ZR, F), BF16),
         dma,
-        dma((C * Y,)),
+        dma((Z,)),
         dma((X - 1,)),
         dma((X - 1,)),
         dma((X - 1,)),
@@ -630,16 +628,15 @@
         dma((6,)),
     ]
     in_vmem = pl.BlockSpec(memory_space=pltpu.VMEM)
-    mesh_out, grad_first, grad_second = pl.pallas_call(
+    mesh_sum, sums = pl.pallas_call(
         functools.partial(kernel, (Z, Y, C, X), scaling),
         out_shape=(
             jax.ShapeDtypeStruct((PATCH, F), BF16),
-            jax.ShapeDtypeStruct((D, F), F32),
-            jax.ShapeDtypeStruct((H, F), F32),
+            jax.ShapeDtypeStruct((C, Z, 2, ZR, F), BF16),
         ),
         in_specs=[pl.BlockSpec(memory_space=pltpu.SMEM)] * 2
         + [pl.BlockSpec(memory_space=pl.ANY)] * 6,
-        out_specs=(in_vmem, in_vmem, in_vmem),
+        out_specs=(in_vmem, in_vmem),
         scratch_shapes=scratch,
         compiler_params=pltpu.CompilerParams(
             collective_id=0, has_side_effects=True, vmem_limit_bytes=62 * 1024 * 1024
@@ -654,7 +651,16 @@
         mlp_second,
         mesh_cotangent,
     )
-    return mesh_out, grad_first, grad_second
+    return pl.pallas_call(
+        hand_out,
+        out_shape=(
+            jax.ShapeDtypeStruct((PATCH, F), BF16),
+            jax.ShapeDtypeStruct((D, F), F32),
+            jax.ShapeDtypeStruct((H, F), F32),
+        ),
+        in_specs=[in_vmem] * 2,
+        out_specs=(in_vmem, in_vmem, in_vmem),
+    )(mesh_sum, sums)
 
 
 def torus_of(mesh):

time: 87.1 us -> 80.3 us (0.922)
  local copies, waits for them, and re-layouts: 3.79 us -> 0 us
  Pallas kernels: 82.4 us -> 79.6 us
    pallas_call x1, Pallas kernels: 82.4 us -> 77.8 us  [per_device(): pl.pallas_call(functools.partial(kernel, (Z, Y, C, X), scaling), out_shap...]
    unnamed x5 -> x0, local copies, waits for them, and re-layouts: 3.79 us -> none
    pallas_call x0 -> x1, Pallas kernels: none -> 1.79 us  [per_device(): pl.pallas_call(hand_out, out_shape=(jax.ShapeDtypeStruct((PATCH, F), BF16...]
where the time goes in v5:
time: 80.3 us; the launch traced here: 80.2 us
  Pallas kernels  79.6 us (99%)
    pallas_call x1, Pallas kernels, per_device(): pl.pallas_call(functools.partial(kernel, (Z, Y, C, X), scaling), out_shap...  77.8 us
    pallas_call x1, Pallas kernels, per_device(): pl.pallas_call(hand_out, out_shape=(jax.ShapeDtypeStruct((PATCH, F), BF16...  1.79 us

profile of v5, /device:TPU:1, one launch (start us, length us, event | category | flops | bytes accessed | tf_op | source)
XLA Modules:
  0.0 80.2 jit_solution(1211314845365209747)
XLA Ops:
  0.6 77.8 %shard_map.103 = (bf16[128,128]{1,0:T(8,128)(2,1)}, bf16[2,8,2,32,128]{4,3,2,1,0:T(8,128)(2,1)}) custom-call(s32[12]{0:T(128)} %source_ref.1, s32[12]{0:T(128)} %live_ref.1, bf16[1024,512]{1,0:T(8,128)(2,1)} %grid_in.1, bf16[128,128]{1,0:T(8,128)(2,1)} %latent_in.1, bf16[12,128,128]{2,1,0:T(8,128)(2,1)} %w_in.1, bf16[512,512]{1,0:T(8,128)(2,1)} %first_in.1, ...), custom_call_target="tpu_custom_call" | custom-call | tf_op jit(solution)/shard_map/pallas_call | solution.py:631
  78.4 1.8 %shard_map.104 = (bf16[128,128]{1,0:T(8,128)(2,1)}, f32[512,128]{1,0:T(8,128)}, f32[512,128]{1,0:T(8,128)}) custom-call(bf16[128,128]{1,0:T(8,128)(2,1)} %get-tuple-element.5.mesh_sum, bf16[2,8,2,32,128]{4,3,2,1,0:T(8,128)(2,1)} %get-tuple-element.6.sums), custom_call_target="tpu_custom_call" | custom-call | tf_op jit(solution)/shard_map/pallas_call | solution.py:654

commit v6 on v5

--- a/solution.py
+++ b/solution.py
@@ -50,6 +50,8 @@
     msg,
     vbig,
     vbig_t,
+    c_own,
+    c_sum,
     c_send,
     c_recv,
     y_send,
@@ -59,6 +61,7 @@
     z_recv,
     x_send,
     x_recv,
+    gm_sum,
     gm,
     gpre,
     gc_send,
@@ -275,7 +278,8 @@
         ).start()
         return carry
 
-    lax.fori_loop(1, NP, send_slot, 0)
+    for dz in near:
+        lax.fori_loop(max(1, dz * Y * 2), (dz + 1) * Y * 2, send_slot, 0)
 
     TR = 2 * PATCH
     T = R // TR
@@ -300,7 +304,7 @@
             arrive(cotb.at[at, c, y, :, pl.ds(0, (X - 1) * F)], cz_r.at[k])
         for m in range(1, Y):
             block = cotb.at[at, c, y]
-            send(block, block, cy_s.at[m - 1, k], cy_r.at[m - 1], patch_1=step(y, m, Y))
+            send(block, block, cy_s.at[m - 1, k], cy_r.at[m - 1, k], patch_1=step(y, m, Y))
 
     loads["grid"].wait()
     loads["first"].wait()
@@ -314,7 +318,6 @@
     for m in range(1, Y):
         to = step(y, m, Y)
         send(metab.at[:, c, y], metab.at[:, c, y], my_s.at[m - 1], my_r.at[m - 1], patch_1=to)
-    send(cotb.at[:, c, y], cotb.at[:, c, y], cc_s.at[0], cc_r.at[0], patch_2=oc)
     own_second.wait()
     for k in range(1, X):
         frm = step(x, X - k, X)
@@ -324,71 +327,76 @@
     for m in range(1, Y):
         arrive(metab.at[:, c, step(y, Y - m, Y)], my_r.at[m - 1])
     send(metab.at[:, c], metab.at[:, c], mc_s.at[0], mc_r.at[0], patch_2=oc)
-    for m in range(1, Y):
-        frm = step(y, Y - m, Y)
-        arrive(cotb.at[:, c, frm], cy_r.at[m - 1])
-        send(cotb.at[:, c, frm], cotb.at[:, c, frm], cc_s.at[m], cc_r.at[m], patch_2=oc)
     arrive(metab.at[:, oc], mc_r.at[0])
 
     own_natural = (z * Y + y) * 2 + c
     PL = C * Y
     TP = PL * PX
-    TC = Z * PX
     lanes = lax.broadcasted_iota(jnp.int32, (PL, PATCH), 1)
 
-    def spread(i, carry):
-        at = lax.rem(z + i, Z)
+    def plane(k):
+        return step(z, (Z - k) % Z, Z)
+
+    def spread(at, slot):
         meta = metab[at].reshape(PL, PATCH)
         patch_of = jnp.sum(jnp.where(lanes == own_natural, meta, 0.0), axis=1, keepdims=True)
         patch_rows = jnp.broadcast_to(
             jnp.broadcast_to(patch_of, (PL, PATCH))[:, None, :], (PL, PX, PATCH)
         ).reshape(TP, PATCH)
         blocks = V[pl.ds(pl.multiple_of(at * PL, PL), PL)].reshape(TP, PATCH).astype(F32)
-        cols = pl.ds(pl.multiple_of(at * TP, TP), TP)
         blocks_t = blocks.T
         patch_cols = patch_rows.T
         for g in range(GPD):
-            part = jnp.where(patch_rows == float(g), blocks, 0.0).astype(BF16)
-            vbig[:, at, :, g * PATCH : (g + 1) * PATCH] = part.reshape(PL, PX, PATCH)
-            vbig_t[g * PATCH : (g + 1) * PATCH, cols] = jnp.where(
+            vbig[:, g * PATCH : (g + 1) * PATCH] = jnp.where(
+                patch_rows == float(g), blocks, 0.0
+            ).astype(BF16)
+            vbig_t[slot, g * PATCH : (g + 1) * PATCH, :] = jnp.where(
                 patch_cols == float(g), blocks_t, 0.0
             ).astype(BF16)
-        return carry
+
+    def contribute(i, k):
+        at, slot = plane(k), i % 2
+        arrive(V.at[pl.ds(0, PL if k else PL - 1)], w_r.at[at])
+        spread(at, slot)
+        c_own[slot] = dot(vbig[...], msg[...]).reshape(C, Y, PX, D)
+        c_send[at] = c_own[slot, oc].astype(BF16)
+        send(c_send.at[at], c_recv.at[at], fc_s.at[k], fc_r.at[k], patch_2=oc)
+        for m in range(1, Y):
+            arrive(cotb.at[at, c, step(y, Y - m, Y)], cy_r.at[m - 1, k])
+        send(cotb.at[at, c], cotb.at[at, c], cc_s.at[k], cc_r.at[k], patch_2=oc)
+
+    def collect(i, k):
+        at, slot = plane(k), i % 2
+        arrive(c_recv.at[at], fc_r.at[k])
+        c_sum[...] = c_own[slot, c] + c_recv[at].astype(F32)
+        y_own[at] = c_sum[y]
+        for m in range(1, Y):
+            to = step(y, m, Y)
+            y_send[m - 1, at] = c_sum[to].astype(BF16)
+            send(
+                y_send.at[m - 1, at],
+                y_recv.at[m - 1, at],
+                fy_s.at[m - 1, k],
+                fy_r.at[m - 1, k],
+                patch_1=to,
+            )
+        arrive(cotb.at[at, oc], cc_r.at[k])
+        for t in range(T):
+            rows = slice(t * TR, (t + 1) * TR)
+            part = dot(vbig_t[slot, rows, :], cotb[at].reshape(TP, D))
+            if i == 0:
+                gm_sum[rows, :] = part
+            elif i < Z - 1:
+                gm_sum[rows, :] += part
+            else:
+                gm[rows, :] = (gm_sum[rows, :] + part).astype(BF16)
 
     own_slot.wait()
-    for k in near:
-        frm = step(z, (Z - k) % Z, Z)
-        arrive(V.at[pl.ds(0, PL if k else PL - 1)], w_r.at[frm])
-        spread((Z - k) % Z, 0)
-
-
-    def contribution(core, yy):
-        return dot(vbig[core * Y + yy].reshape(TC, R), msg[...])
-
-    for k in range(1, Y + 1):
-        yy = step(y, k % Y, Y)
-        c_send[yy] = contribution(oc, yy).astype(BF16).reshape(Z, PX, D)
-        send(c_send.at[yy], c_recv.at[yy], fc_s.at[k - 1], fc_r.at[k - 1], patch_2=oc)
-    for k in range(1, Y + 1):
-        yy = step(y, k % Y, Y)
-        part = contribution(c, yy)
-        arrive(c_recv.at[yy], fc_r.at[k - 1])
-        part = part + c_recv[yy].astype(F32).reshape(TC, D)
-        if k < Y:
-            y_send[k - 1] = part.astype(BF16).reshape(Z, PX, D)
-            send(y_send.at[k - 1], y_recv.at[k - 1], fy_s.at[k - 1], fy_r.at[k - 1], patch_1=yy)
-        else:
-            y_own[...] = part.reshape(Z, PX, D)
-
-    for m in range(Y):
-        arrive(cotb.at[:, oc, step(y, Y - m, Y)], cc_r.at[m])
-
-    def message_gradient(i, carry):
-        rows = pl.ds(pl.multiple_of(i * TR, TR), TR)
-        gm[rows, :] = dot(vbig_t[rows, :], cotb[...].reshape(NP * PX, D)).astype(BF16)
-        return carry
-
-    lax.fori_loop(0, R // TR, message_gradient, 0)
+    for i, k in enumerate(near):
+        contribute(i, k)
+        if i:
+            collect(i - 1, near[i - 1])
+    collect(Z - 1, near[-1])
 
     def halves(which, left_ref, right_ref):
         for core in (oc, c):
@@ -438,6 +446,18 @@
 
     over_mp(1)
 
+    for k in near:
+        at = plane(k)
+        total = y_own[at]
+        for m in range(1, Y):
+            arrive(y_recv.at[m - 1, at], fy_r.at[m - 1, k])
+            total = total + y_recv[m - 1, at].astype(F32)
+        if k:
+            z_send[at] = total.astype(BF16)
+            send(z_send.at[at], z_recv.at[k - 1], fz_s.at[k - 1], fz_r.at[k - 1], patch_0=at)
+        else:
+            y_own[at] = total
+
     ZR = HC // Z
     for which in range(2):
         total = g_own[which, x]
@@ -449,17 +469,6 @@
     for k in range(1, Z):
         to = step(z, k, Z)
         send(gz_send.at[to], gz_recv.at[k - 1], gz_s.at[k - 1], gz_r.at[k - 1], patch_0=to)
-
-    for k in range(1, Y):
-        arrive(y_recv.at[k - 1], fy_r.at[k - 1])
-    total = y_own[...]
-    for k in range(1, Y):
-        total = total + y_recv[k - 1].astype(F32)
-    y_own[...] = total
-    z_send[...] = total.astype(BF16)
-    for k in range(1, Z):
-        to = step(z, k, Z)
-        send(z_send.at[to], z_recv.at[k - 1], fz_s.at[k - 1], fz_r.at[k - 1], patch_0=to)
 
     total = g_own[:, x, pl.ds(pl.multiple_of(z * ZR, ZR), ZR)]
     for k in range(1, Z):
@@ -564,10 +573,12 @@
         vm((R, H), F32),
         vm((R, H), BF16),
         vm((R, D), BF16),
-        vm((C * Y, Z, PX, R), BF16),
-        vm((R, NP * PX), BF16),
-        vm((Y, Z, PX, D), BF16),
-        vm((Y, Z, PX, D), BF16),
+        vm((C * Y * PX, R), BF16),
+        vm((2, R, C * Y * PX), BF16),
+        vm((2, C, Y, PX, D), F32),
+        vm((Y, PX, D), F32),
+        vm((Z, Y, PX, D), BF16),
+        vm((Z, Y, PX, D), BF16),
         vm((Y - 1, Z, PX, D), BF16),
         vm((Y - 1, Z, PX, D), BF16),
         vm((Z, PX, D), F32),
@@ -575,6 +586,7 @@
         vm((Z - 1, PX, D), BF16),
         vm((X, PX, F), F32),
         vm((X, PX, F), F32),
+        vm((R, D), F32),
         vm((R, D), BF16),
         vm((R, H), BF16),
         vm((2, X, HC, F), F32),
@@ -595,19 +607,19 @@
         dma((Z, X)),
         dma((Z,)),
         dma((Y - 1, Z)),
-        dma((Y - 1,)),
-        dma((4,)),
-        dma((4,)),
+        dma((Y - 1, Z)),
+        dma((Z,)),
+        dma((Z,)),
         dma((Z - 1,)),
         dma((Z - 1,)),
         dma((Y - 1,)),
         dma((Y - 1,)),
         dma((1,)),
         dma((1,)),
-        dma((Y,)),
-        dma((Y,)),
-        dma((Y - 1,)),
-        dma((Y - 1,)),
+        dma((Z,)),
+        dma((Z,)),
+        dma((Y - 1, Z)),
+        dma((Y - 1, Z)),
         dma((Z - 1,)),
         dma((Z - 1,)),
         dma((X - 1,)),

time: 80.3 us -> 81.4 us (1.014)
  Pallas kernels: 79.6 us -> 80.7 us
    pallas_call x1, Pallas kernels: 77.8 us -> 78.9 us  [per_device(): pl.pallas_call(functools.partial(kernel, (Z, Y, C, X), scaling), out_shap...]
where the time goes in v6:
time: 81.4 us; the launch traced here: 81.3 us
  Pallas kernels  80.7 us (99%)
    pallas_call x1, Pallas kernels, per_device(): pl.pallas_call(functools.partial(kernel, (Z, Y, C, X), scaling), out_shap...  78.9 us
    pallas_call x1, Pallas kernels, per_device(): pl.pallas_call(hand_out, out_shape=(jax.ShapeDtypeStruct((PATCH, F), BF16...  1.79 us

profile of v6, /device:TPU:1, one launch (start us, length us, event | category | flops | bytes accessed | tf_op | source)
XLA Modules:
  0.0 81.3 jit_solution(7871527485225278630)
XLA Ops:
  0.6 78.9 %shard_map.103 = (bf16[128,128]{1,0:T(8,128)(2,1)}, bf16[2,8,2,32,128]{4,3,2,1,0:T(8,128)(2,1)}) custom-call(s32[12]{0:T(128)} %source_ref.1, s32[12]{0:T(128)} %live_ref.1, bf16[1024,512]{1,0:T(8,128)(2,1)} %grid_in.1, bf16[128,128]{1,0:T(8,128)(2,1)} %latent_in.1, bf16[12,128,128]{2,1,0:T(8,128)(2,1)} %w_in.1, bf16[512,512]{1,0:T(8,128)(2,1)} %first_in.1, ...), custom_call_target="tpu_custom_call" | custom-call | tf_op jit(solution)/shard_map/pallas_call | solution.py:643
  79.5 1.8 %shard_map.104 = (bf16[128,128]{1,0:T(8,128)(2,1)}, f32[512,128]{1,0:T(8,128)}, f32[512,128]{1,0:T(8,128)}) custom-call(bf16[128,128]{1,0:T(8,128)(2,1)} %get-tuple-element.5.mesh_sum, bf16[2,8,2,32,128]{4,3,2,1,0:T(8,128)(2,1)} %get-tuple-element.6.sums), custom_call_target="tpu_custom_call" | custom-call | tf_op jit(solution)/shard_map/pallas_call | solution.py:666

commit v7 on v6

--- a/solution.py
+++ b/solution.py
@@ -89,8 +89,6 @@
     mz_r,
     my_s,
     my_r,
-    mc_s,
-    mc_r,
     fc_s,
     fc_r,
     fy_s,
@@ -240,6 +238,14 @@
     near = [0]
     for t in range(1, Z // 2 + 1):
         near += [t, Z - t] if 2 * t < Z else [t]
+    for k in near[1:]:
+        send(
+            metab.at[z, c, y],
+            metab.at[z, c, y],
+            mz_s.at[k - 1],
+            mz_r.at[k - 1],
+            patch_0=step(z, k, Z),
+        )
     for k in near:
         for m in range(X):
             if k or m:
@@ -253,14 +259,6 @@
                     patch_0=step(z, k, Z),
                     mp=to,
                 )
-        if k:
-            send(
-                metab.at[z, c, y],
-                metab.at[z, c, y],
-                mz_s.at[k - 1],
-                mz_r.at[k - 1],
-                patch_0=step(z, k, Z),
-            )
     for k in range(1, X):
         to = step(x, k, X)
         send(second_ref, second.at[:, xf], sec_s.at[k - 1], sec_r.at[k - 1], mp=to)
@@ -313,21 +311,27 @@
         first_layer(i)
         for k in near[i * per : (i + 1) * per]:
             over_y(k)
-    for k in range(1, Z):
-        arrive(metab.at[step(z, Z - k, Z), c, y], mz_r.at[k - 1])
-    for m in range(1, Y):
-        to = step(y, m, Y)
-        send(metab.at[:, c, y], metab.at[:, c, y], my_s.at[m - 1], my_r.at[m - 1], patch_1=to)
+        if i == 0:
+            for k in range(1, Z):
+                arrive(metab.at[step(z, Z - k, Z), c, y], mz_r.at[k - 1])
+            for j in range(1, 2 * Y):
+                send(
+                    metab.at[:, c, y],
+                    metab.at[:, c, y],
+                    my_s.at[j],
+                    my_r.at[j],
+                    patch_1=step(y, j // 2, Y),
+                    patch_2=lax.rem(c + j % 2, 2),
+                )
     own_second.wait()
     for k in range(1, X):
         frm = step(x, X - k, X)
         arrive(second.at[:, pl.ds(pl.multiple_of(frm * F, F), F)], sec_r.at[k - 1])
     for i in range(T):
         second_layer(i)
-    for m in range(1, Y):
-        arrive(metab.at[:, c, step(y, Y - m, Y)], my_r.at[m - 1])
-    send(metab.at[:, c], metab.at[:, c], mc_s.at[0], mc_r.at[0], patch_2=oc)
-    arrive(metab.at[:, oc], mc_r.at[0])
+    for j in range(1, 2 * Y):
+        core, yy = lax.rem(c + j % 2, 2), step(y, Y - j // 2, Y)
+        arrive(metab.at[:, core, yy], my_r.at[j])
 
     own_natural = (z * Y + y) * 2 + c
     PL = C * Y
@@ -612,10 +616,8 @@
         dma((Z,)),
         dma((Z - 1,)),
         dma((Z - 1,)),
-        dma((Y - 1,)),
-        dma((Y - 1,)),
-        dma((1,)),
-        dma((1,)),
+        dma((2 * Y,)),
+        dma((2 * Y,)),
         dma((Z,)),
         dma((Z,)),
         dma((Y - 1, Z)),

time: 81.4 us -> 75 us (0.921)
  Pallas kernels: 80.7 us -> 74.2 us
    pallas_call x1, Pallas kernels: 78.9 us -> 72.4 us  [per_device(): pl.pallas_call(functools.partial(kernel, (Z, Y, C, X), scaling), out_shap...]
where the time goes in v7:
time: 75 us; the launch traced here: 74.9 us
  Pallas kernels  74.2 us (99%)
    pallas_call x1, Pallas kernels, per_device(): pl.pallas_call(functools.partial(kernel, (Z, Y, C, X), scaling), out_shap...  72.4 us
    pallas_call x1, Pallas kernels, per_device(): pl.pallas_call(hand_out, out_shape=(jax.ShapeDtypeStruct((PATCH, F), BF16...  1.79 us

profile of v7, /device:TPU:1, one launch (start us, length us, event | category | flops | bytes accessed | tf_op | source)
XLA Modules:
  0.0 74.9 jit_solution(2843866146077983245)
XLA Ops:
  0.6 72.4 %shard_map.103 = (bf16[128,128]{1,0:T(8,128)(2,1)}, bf16[2,8,2,32,128]{4,3,2,1,0:T(8,128)(2,1)}) custom-call(s32[12]{0:T(128)} %source_ref.1, s32[12]{0:T(128)} %live_ref.1, bf16[1024,512]{1,0:T(8,128)(2,1)} %grid_in.1, bf16[128,128]{1,0:T(8,128)(2,1)} %latent_in.1, bf16[12,128,128]{2,1,0:T(8,128)(2,1)} %w_in.1, bf16[512,512]{1,0:T(8,128)(2,1)} %first_in.1, ...), custom_call_target="tpu_custom_call" | custom-call | tf_op jit(solution)/shard_map/pallas_call | solution.py:645
  73.1 1.8 %shard_map.104 = (bf16[128,128]{1,0:T(8,128)(2,1)}, f32[512,128]{1,0:T(8,128)}, f32[512,128]{1,0:T(8,128)}) custom-call(bf16[128,128]{1,0:T(8,128)(2,1)} %get-tuple-element.5.mesh_sum, bf16[2,8,2,32,128]{4,3,2,1,0:T(8,128)(2,1)} %get-tuple-element.6.sums), custom_call_target="tpu_custom_call" | custom-call | tf_op jit(solution)/shard_map/pallas_call | solution.py:668

commit v8 on v7

--- a/solution.py
+++ b/solution.py
@@ -225,7 +225,9 @@
     loads["second"].wait()
     own_cot = pltpu.make_async_copy(cot_ref.at[xp, :], cotb.at[z, c, y, :, xf], loc.at[0])
     own_cot.start()
-    own_second = pltpu.make_async_copy(second_ref, second.at[:, xf], loc.at[1])
+    half = pl.ds(pl.multiple_of(c * (H // 2), H // 2), H // 2)
+    other_half = pl.ds(pl.multiple_of(oc * (H // 2), H // 2), H // 2)
+    own_second = pltpu.make_async_copy(second_ref.at[half], second.at[half, xf], loc.at[1])
     own_second.start()
     own_meta = pltpu.make_async_copy(meta_ref, metab.at[z, c, y], loc.at[2])
     own_meta.start()
@@ -261,7 +263,9 @@
                 )
     for k in range(1, X):
         to = step(x, k, X)
-        send(second_ref, second.at[:, xf], sec_s.at[k - 1], sec_r.at[k - 1], mp=to)
+        send(
+            second_ref.at[half], second.at[half, xf], sec_s.at[k - 1], sec_r.at[k - 1], mp=to
+        )
 
     def send_slot(j, carry):
         dz, dy, dc = j // (Y * 2), (j // 2) % Y, j % 2
@@ -326,7 +330,9 @@
     own_second.wait()
     for k in range(1, X):
         frm = step(x, X - k, X)
-        arrive(second.at[:, pl.ds(pl.multiple_of(frm * F, F), F)], sec_r.at[k - 1])
+        arrive(second.at[half, pl.ds(pl.multiple_of(frm * F, F), F)], sec_r.at[k - 1])
+    send(second.at[half], second.at[half], sec_s.at[X - 1], sec_r.at[X - 1], patch_2=oc)
+    arrive(second.at[other_half], sec_r.at[X - 1])
     for i in range(T):
         second_layer(i)
     for j in range(1, 2 * Y):
@@ -337,6 +343,9 @@
     PL = C * Y
     TP = PL * PX
     lanes = lax.broadcasted_iota(jnp.int32, (PL, PATCH), 1)
+    of_receiver = lax.broadcasted_iota(jnp.int32, (PL, TP), 1) // PX == lax.broadcasted_iota(
+        jnp.int32, (PL, TP), 0
+    )
 
     def plane(k):
         return step(z, (Z - k) % Z, Z)
@@ -344,19 +353,22 @@
     def spread(at, slot):
         meta = metab[at].reshape(PL, PATCH)
         patch_of = jnp.sum(jnp.where(lanes == own_natural, meta, 0.0), axis=1, keepdims=True)
-        patch_rows = jnp.broadcast_to(
-            jnp.broadcast_to(patch_of, (PL, PATCH))[:, None, :], (PL, PX, PATCH)
-        ).reshape(TP, PATCH)
+        patch_rows = jnp.broadcast_to(jnp.broadcast_to(patch_of, (PL, PATCH))[:, None], (PL, 8, PATCH))
+        patch_cols = jnp.sum(
+            jnp.where(of_receiver, jnp.broadcast_to(patch_of, (PL, TP)), 0.0),
+            axis=0,
+            keepdims=True,
+        )
         blocks = V[pl.ds(pl.multiple_of(at * PL, PL), PL)].reshape(TP, PATCH).astype(F32)
         blocks_t = blocks.T
-        patch_cols = patch_rows.T
+        tiles = blocks.reshape(PL, PX // 8, 8, PATCH)
         for g in range(GPD):
-            vbig[:, g * PATCH : (g + 1) * PATCH] = jnp.where(
-                patch_rows == float(g), blocks, 0.0
-            ).astype(BF16)
-            vbig_t[slot, g * PATCH : (g + 1) * PATCH, :] = jnp.where(
-                patch_cols == float(g), blocks_t, 0.0
-            ).astype(BF16)
+            in_rows = jnp.where(patch_rows == float(g), 1.0, 0.0)
+            vbig[:, g * PATCH : (g + 1) * PATCH] = (
+                (tiles * in_rows[:, None]).reshape(TP, PATCH).astype(BF16)
+            )
+            in_cols = jnp.where(patch_cols == float(g), 1.0, 0.0)
+            vbig_t[slot, g * PATCH : (g + 1) * PATCH, :] = (blocks_t * in_cols).astype(BF16)
 
     def contribute(i, k):
         at, slot = plane(k), i % 2
@@ -604,8 +616,8 @@
         vm((2, ZR, F), BF16),
         dma,
         dma((Z,)),
-        dma((X - 1,)),
-        dma((X - 1,)),
+        dma((X,)),
+        dma((X,)),
         dma((X - 1,)),
         dma((X - 1,)),
         dma((Z, X)),

time: 75 us -> 75 us (level)
  no operation moved by 1% of the time
where the time goes in v8:
time: 75 us; the launch traced here: 74.8 us
  Pallas kernels  74.2 us (99%)
    pallas_call x1, Pallas kernels, per_device(): pl.pallas_call(functools.partial(kernel, (Z, Y, C, X), scaling), out_shap...  72.4 us
    pallas_call x1, Pallas kernels, per_device(): pl.pallas_call(hand_out, out_shape=(jax.ShapeDtypeStruct((PATCH, F), BF16...  1.79 us

profile of v8, /device:TPU:1, one launch (start us, length us, event | category | flops | bytes accessed | tf_op | source)
XLA Modules:
  0.0 74.8 jit_solution(13917709876072058456)
XLA Ops:
  0.6 72.4 %shard_map.103 = (bf16[128,128]{1,0:T(8,128)(2,1)}, bf16[2,8,2,32,128]{4,3,2,1,0:T(8,128)(2,1)}) custom-call(s32[12]{0:T(128)} %source_ref.1, s32[12]{0:T(128)} %live_ref.1, bf16[1024,512]{1,0:T(8,128)(2,1)} %grid_in.1, bf16[128,128]{1,0:T(8,128)(2,1)} %latent_in.1, bf16[12,128,128]{2,1,0:T(8,128)(2,1)} %w_in.1, bf16[512,512]{1,0:T(8,128)(2,1)} %first_in.1, ...), custom_call_target="tpu_custom_call" | custom-call | tf_op jit(solution)/shard_map/pallas_call | solution.py:657
  73.1 1.8 %shard_map.104 = (bf16[128,128]{1,0:T(8,128)(2,1)}, f32[512,128]{1,0:T(8,128)}, f32[512,128]{1,0:T(8,128)}) custom-call(bf16[128,128]{1,0:T(8,128)(2,1)} %get-tuple-element.5.mesh_sum, bf16[2,8,2,32,128]{4,3,2,1,0:T(8,128)(2,1)} %get-tuple-element.6.sums), custom_call_target="tpu_custom_call" | custom-call | tf_op jit(solution)/shard_map/pallas_call | solution.py:680

commit v9 on v8

--- a/solution.py
+++ b/solution.py
@@ -206,21 +206,6 @@
         inside = lax.rem(source_ref[j], GPD).astype(F32)
         meta = jnp.where(lane == feeder(j), inside, meta)
     meta_ref[...] = meta
-    loads["w"].wait()
-
-    def pack(i, carry):
-        z1, c1, y1 = i // (2 * Y), (i // Y) % 2, i % Y
-        natural = (z1 * Y + y1) * 2 + c1
-        slot, live = jnp.int32(0), jnp.int32(0)
-        for j in range(n_slots):
-            hit = feeder(j) == natural
-            slot = jnp.where(hit, j, slot)
-            live = jnp.where(hit, 1, live)
-        block = w_ref[slot, xp, :]
-        slots[i] = (block.astype(F32) * live.astype(F32)).astype(BF16)
-        return carry
-
-    lax.fori_loop(0, NP, pack, 0)
     loads["cot"].wait()
     loads["second"].wait()
     own_cot = pltpu.make_async_copy(cot_ref.at[xp, :], cotb.at[z, c, y, :, xf], loc.at[0])
@@ -232,8 +217,6 @@
     own_meta = pltpu.make_async_copy(meta_ref, metab.at[z, c, y], loc.at[2])
     own_meta.start()
     here = (z * 2 + c) * Y + y
-    own_slot = pltpu.make_async_copy(slots.at[here], V.at[here], loc.at[3])
-    own_slot.start()
     pl.semaphore_wait(barrier, NP - 1 + (X - 1) * Z)
 
     own_meta.wait()
@@ -267,6 +250,24 @@
             second_ref.at[half], second.at[half, xf], sec_s.at[k - 1], sec_r.at[k - 1], mp=to
         )
 
+    loads["w"].wait()
+
+    def pack(i, carry):
+        z1, c1, y1 = i // (2 * Y), (i // Y) % 2, i % Y
+        natural = (z1 * Y + y1) * 2 + c1
+        slot, live = jnp.int32(0), jnp.int32(0)
+        for j in range(n_slots):
+            hit = feeder(j) == natural
+            slot = jnp.where(hit, j, slot)
+            live = jnp.where(hit, 1, live)
+        block = w_ref[slot, xp, :]
+        slots[i] = (block.astype(F32) * live.astype(F32)).astype(BF16)
+        return carry
+
+    lax.fori_loop(0, NP, pack, 0)
+    own_slot = pltpu.make_async_copy(slots.at[here], V.at[here], loc.at[3])
+    own_slot.start()
+
     def send_slot(j, carry):
         dz, dy, dc = j // (Y * 2), (j // 2) % Y, j % 2
         z1, y1, c1 = lax.rem(z + dz, Z), lax.rem(y + dy, Y), lax.rem(c + dc, 2)
@@ -462,6 +463,18 @@
 
     over_mp(1)
 
+    ZR = HC // Z
+    for which in range(2):
+        total = g_own[which, x]
+        for k in range(1, X):
+            arrive(gx_recv.at[which, k - 1], gx_r.at[which, k - 1])
+            total = total + gx_recv[which, k - 1].astype(F32)
+        g_own[which, x] = total
+        gz_send[:, which] = total.reshape(Z, ZR, F).astype(BF16)
+    for k in range(1, Z):
+        to = step(z, k, Z)
+        send(gz_send.at[to], gz_recv.at[k - 1], gz_s.at[k - 1], gz_r.at[k - 1], patch_0=to)
+
     for k in near:
         at = plane(k)
         total = y_own[at]
@@ -473,18 +486,6 @@
             send(z_send.at[at], z_recv.at[k - 1], fz_s.at[k - 1], fz_r.at[k - 1], patch_0=at)
         else:
             y_own[at] = total
-
-    ZR = HC // Z
-    for which in range(2):
-        total = g_own[which, x]
-        for k in range(1, X):
-            arrive(gx_recv.at[which, k - 1], gx_r.at[which, k - 1])
-            total = total + gx_recv[which, k - 1].astype(F32)
-        g_own[which, x] = total
-        gz_send[:, which] = total.reshape(Z, ZR, F).astype(BF16)
-    for k in range(1, Z):
-        to = step(z, k, Z)
-        send(gz_send.at[to], gz_recv.at[k - 1], gz_s.at[k - 1], gz_r.at[k - 1], patch_0=to)
 
     total = g_own[:, x, pl.ds(pl.multiple_of(z * ZR, ZR), ZR)]
     for k in range(1, Z):

time: 75 us -> 75.7 us (level)
  no operation moved by 1% of the time
where the time goes in v9:
time: 75.7 us; the launch traced here: 75.6 us
  Pallas kernels  74.9 us (99%)
    pallas_call x1, Pallas kernels, per_device(): pl.pallas_call(functools.partial(kernel, (Z, Y, C, X), scaling), out_shap...  73.1 us
    pallas_call x1, Pallas kernels, per_device(): pl.pallas_call(hand_out, out_shape=(jax.ShapeDtypeStruct((PATCH, F), BF16...  1.79 us

profile of v9, /device:TPU:1, one launch (start us, length us, event | category | flops | bytes accessed | tf_op | source)
XLA Modules:
  0.0 75.6 jit_solution(16619691592517269278)
XLA Ops:
  0.6 73.1 %shard_map.103 = (bf16[128,128]{1,0:T(8,128)(2,1)}, bf16[2,8,2,32,128]{4,3,2,1,0:T(8,128)(2,1)}) custom-call(s32[12]{0:T(128)} %source_ref.1, s32[12]{0:T(128)} %live_ref.1, bf16[1024,512]{1,0:T(8,128)(2,1)} %grid_in.1, bf16[128,128]{1,0:T(8,128)(2,1)} %latent_in.1, bf16[12,128,128]{2,1,0:T(8,128)(2,1)} %w_in.1, bf16[512,512]{1,0:T(8,128)(2,1)} %first_in.1, ...), custom_call_target="tpu_custom_call" | custom-call | tf_op jit(solution)/shard_map/pallas_call | solution.py:658
  73.8 1.8 %shard_map.104 = (bf16[128,128]{1,0:T(8,128)(2,1)}, f32[512,128]{1,0:T(8,128)}, f32[512,128]{1,0:T(8,128)}) custom-call(bf16[128,128]{1,0:T(8,128)(2,1)} %get-tuple-element.5.mesh_sum, bf16[2,8,2,32,128]{4,3,2,1,0:T(8,128)(2,1)} %get-tuple-element.6.sums), custom_call_target="tpu_custom_call" | custom-call | tf_op jit(solution)/shard_map/pallas_call | solution.py:681

commit v10 on v8

--- a/solution.py
+++ b/solution.py
@@ -81,6 +81,7 @@
     cx_r,
     cz_s,
     cz_r,
+    ch_r,
     cy_s,
     cy_r,
     cc_s,
@@ -248,9 +249,10 @@
             mz_r.at[k - 1],
             patch_0=step(z, k, Z),
         )
+    relayed = (3, 4, 5) if Z == 8 else ()
     for k in near:
         for m in range(X):
-            if k or m:
+            if k not in relayed and (k or m):
                 to = step(x, m, X)
                 rows = pl.ds(pl.multiple_of(to * PX, PX), PX)
                 send(
@@ -299,13 +301,21 @@
 
     def over_y(k):
         at = step(z, (Z - k) % Z, Z)
-        if k:
+        halves_of = [cotb.at[at, c, y, pl.ds(h * (PX // 2), PX // 2)] for h in range(2)]
+        if relayed and k == 4:
+            for h in range(2):
+                arrive(halves_of[h], ch_r.at[h])
+        elif k:
             arrive(cotb.at[at, c, y], cz_r.at[k])
         else:
             own_cot.wait()
             arrive(cotb.at[at, c, y, :, pl.ds(0, (X - 1) * F)], cz_r.at[k])
+        block = cotb.at[at, c, y]
+        if relayed and k in (2, Z - 2):
+            h, far, one, two = (0, 3, 1, 2) if k == 2 else (1, 5, Z - 1, Z - 2)
+            send(block, block, cz_s.at[far, 0], cz_r.at[far], patch_0=step(z, one, Z))
+            send(halves_of[h], halves_of[h], cz_s.at[far, 1], ch_r.at[h], patch_0=step(z, two, Z))
         for m in range(1, Y):
-            block = cotb.at[at, c, y]
             send(block, block, cy_s.at[m - 1, k], cy_r.at[m - 1, k], patch_1=step(y, m, Y))
 
     loads["grid"].wait()
@@ -622,6 +632,7 @@
         dma((X - 1,)),
         dma((Z, X)),
         dma((Z,)),
+        dma((2,)),
         dma((Y - 1, Z)),
         dma((Y - 1, Z)),
         dma((Z,)),

time: 75 us -> 78.7 us (1.049)
  Pallas kernels: 74.2 us -> 77.9 us
    pallas_call x1, Pallas kernels: 72.4 us -> 76.1 us  [per_device(): pl.pallas_call(functools.partial(kernel, (Z, Y, C, X), scaling), out_shap...]
where the time goes in v10:
time: 78.7 us; the launch traced here: 78.6 us
  Pallas kernels  77.9 us (99%)
    pallas_call x1, Pallas kernels, per_device(): pl.pallas_call(functools.partial(kernel, (Z, Y, C, X), scaling), out_shap...  76.1 us
    pallas_call x1, Pallas kernels, per_device(): pl.pallas_call(hand_out, out_shape=(jax.ShapeDtypeStruct((PATCH, F), BF16...  1.79 us

profile of v10, /device:TPU:1, one launch (start us, length us, event | category | flops | bytes accessed | tf_op | source)
XLA Modules:
  0.0 78.6 jit_solution(10110801805616765028)
XLA Ops:
  0.6 76.1 %shard_map.103 = (bf16[128,128]{1,0:T(8,128)(2,1)}, bf16[2,8,2,32,128]{4,3,2,1,0:T(8,128)(2,1)}) custom-call(s32[12]{0:T(128)} %source_ref.1, s32[12]{0:T(128)} %live_ref.1, bf16[1024,512]{1,0:T(8,128)(2,1)} %grid_in.1, bf16[128,128]{1,0:T(8,128)(2,1)} %latent_in.1, bf16[12,128,128]{2,1,0:T(8,128)(2,1)} %w_in.1, bf16[512,512]{1,0:T(8,128)(2,1)} %first_in.1, ...), custom_call_target="tpu_custom_call" | custom-call | tf_op jit(solution)/shard_map/pallas_call | solution.py:668
  76.8 1.8 %shard_map.104 = (bf16[128,128]{1,0:T(8,128)(2,1)}, f32[512,128]{1,0:T(8,128)}, f32[512,128]{1,0:T(8,128)}) custom-call(bf16[128,128]{1,0:T(8,128)(2,1)} %get-tuple-element.5.mesh_sum, bf16[2,8,2,32,128]{4,3,2,1,0:T(8,128)(2,1)} %get-tuple-element.6.sums), custom_call_target="tpu_custom_call" | custom-call | tf_op jit(solution)/shard_map/pallas_call | solution.py:691

commit v11 on v8

--- a/solution.py
+++ b/solution.py
@@ -280,8 +280,9 @@
         ).start()
         return carry
 
-    for dz in near:
-        lax.fori_loop(max(1, dz * Y * 2), (dz + 1) * Y * 2, send_slot, 0)
+    def send_planes(planes):
+        for dz in planes:
+            lax.fori_loop(max(1, dz * Y * 2), (dz + 1) * Y * 2, send_slot, 0)
 
     TR = 2 * PATCH
     T = R // TR
@@ -311,10 +312,12 @@
     loads["grid"].wait()
     loads["first"].wait()
     per = -(-Z // T)
+    send_planes(near[:per])
     for i in range(T):
         first_layer(i)
         for k in near[i * per : (i + 1) * per]:
             over_y(k)
+        send_planes(near[(i + 1) * per : (i + 2) * per])
         if i == 0:
             for k in range(1, Z):
                 arrive(metab.at[step(z, Z - k, Z), c, y], mz_r.at[k - 1])

time: 75 us -> 75.3 us (level)
  no operation moved by 1% of the time
where the time goes in v11:
time: 75.3 us; the launch traced here: 75.2 us
  Pallas kernels  74.6 us (99%)
    pallas_call x1, Pallas kernels, per_device(): pl.pallas_call(functools.partial(kernel, (Z, Y, C, X), scaling), out_shap...  72.8 us
    pallas_call x1, Pallas kernels, per_device(): pl.pallas_call(hand_out, out_shape=(jax.ShapeDtypeStruct((PATCH, F), BF16...  1.79 us

profile of v11, /device:TPU:1, one launch (start us, length us, event | category | flops | bytes accessed | tf_op | source)
XLA Modules:
  0.0 75.2 jit_solution(16435935526783246706)
XLA Ops:
  0.6 72.8 %shard_map.103 = (bf16[128,128]{1,0:T(8,128)(2,1)}, bf16[2,8,2,32,128]{4,3,2,1,0:T(8,128)(2,1)}) custom-call(s32[12]{0:T(128)} %source_ref.1, s32[12]{0:T(128)} %live_ref.1, bf16[1024,512]{1,0:T(8,128)(2,1)} %grid_in.1, bf16[128,128]{1,0:T(8,128)(2,1)} %latent_in.1, bf16[12,128,128]{2,1,0:T(8,128)(2,1)} %w_in.1, bf16[512,512]{1,0:T(8,128)(2,1)} %first_in.1, ...), custom_call_target="tpu_custom_call" | custom-call | tf_op jit(solution)/shard_map/pallas_call | solution.py:660
  73.4 1.8 %shard_map.104 = (bf16[128,128]{1,0:T(8,128)(2,1)}, f32[512,128]{1,0:T(8,128)}, f32[512,128]{1,0:T(8,128)}) custom-call(bf16[128,128]{1,0:T(8,128)(2,1)} %get-tuple-element.5.mesh_sum, bf16[2,8,2,32,128]{4,3,2,1,0:T(8,128)(2,1)} %get-tuple-element.6.sums), custom_call_target="tpu_custom_call" | custom-call | tf_op jit(solution)/shard_map/pallas_call | solution.py:683

commit v12 on v7

--- a/solution.py
+++ b/solution.py
@@ -402,24 +402,20 @@
             collect(i - 1, near[i - 1])
     collect(Z - 1, near[-1])
 
-    def halves(which, left_ref, right_ref):
-        for core in (oc, c):
-            cols = pl.ds(pl.multiple_of(core * HC, HC), HC)
-            part = dot(left_ref[:, cols], right_ref[...], ((0,), (0,))) * scaling
-            for q in range(X):
-                piece = part[:, q * F : (q + 1) * F]
-                if core is oc:
-                    gc_send[which, q] = piece
-                else:
-                    g_own[which, q] = piece
-            if core is oc:
-                send(
-                    gc_send.at[which],
-                    gc_recv.at[which],
-                    gc_s.at[which],
-                    gc_r.at[which],
-                    patch_2=oc,
-                )
+    def half_of(core, which, left_ref, right_ref, into):
+        cols = pl.ds(pl.multiple_of(core * HC, HC), HC)
+        part = dot(left_ref[:, cols], right_ref[...], ((0,), (0,))) * scaling
+        for q in range(X):
+            into[which, q] = part[:, q * F : (q + 1) * F]
+
+    def give(which, left_ref, right_ref):
+        half_of(oc, which, left_ref, right_ref, gc_send)
+        send(
+            gc_send.at[which], gc_recv.at[which], gc_s.at[which], gc_r.at[which], patch_2=oc
+        )
+
+    def keep(which, left_ref, right_ref):
+        half_of(c, which, left_ref, right_ref, g_own)
 
     def over_mp(which):
         arrive(gc_recv.at[which], gc_r.at[which])
@@ -435,7 +431,7 @@
             )
         g_own[which, x] = g_own[which, x] + gc_recv[which, x]
 
-    halves(0, hidden, gm)
+    give(0, hidden, gm)
 
     def pre_gradient(i, carry):
         rows = pl.ds(pl.multiple_of(i * TR, TR), TR)
@@ -444,9 +440,10 @@
         return carry
 
     lax.fori_loop(0, R // TR, pre_gradient, 0)
+    give(1, grid_ref, gpre)
+    keep(0, hidden, gm)
     over_mp(0)
-
-    halves(1, grid_ref, gpre)
+    keep(1, grid_ref, gpre)
 
     over_mp(1)
 

time: 75 us -> 74.9 us (level)
  no operation moved by 1% of the time
where the time goes in v12:
time: 74.9 us; the launch traced here: 74.8 us
  Pallas kernels  74.2 us (99%)
    pallas_call x1, Pallas kernels, per_device(): pl.pallas_call(functools.partial(kernel, (Z, Y, C, X), scaling), out_shap...  72.4 us
    pallas_call x1, Pallas kernels, per_device(): pl.pallas_call(hand_out, out_shape=(jax.ShapeDtypeStruct((PATCH, F), BF16...  1.79 us

profile of v12, /device:TPU:1, one launch (start us, length us, event | category | flops | bytes accessed | tf_op | source)
XLA Modules:
  0.0 74.8 jit_solution(9587360751323721792)
XLA Ops:
  0.6 72.4 %shard_map.103 = (bf16[128,128]{1,0:T(8,128)(2,1)}, bf16[2,8,2,32,128]{4,3,2,1,0:T(8,128)(2,1)}) custom-call(s32[12]{0:T(128)} %source_ref.1, s32[12]{0:T(128)} %live_ref.1, bf16[1024,512]{1,0:T(8,128)(2,1)} %grid_in.1, bf16[128,128]{1,0:T(8,128)(2,1)} %latent_in.1, bf16[12,128,128]{2,1,0:T(8,128)(2,1)} %w_in.1, bf16[512,512]{1,0:T(8,128)(2,1)} %first_in.1, ...), custom_call_target="tpu_custom_call" | custom-call | tf_op jit(solution)/shard_map/pallas_call | solution.py:642
  73.0 1.8 %shard_map.104 = (bf16[128,128]{1,0:T(8,128)(2,1)}, f32[512,128]{1,0:T(8,128)}, f32[512,128]{1,0:T(8,128)}) custom-call(bf16[128,128]{1,0:T(8,128)(2,1)} %get-tuple-element.5.mesh_sum, bf16[2,8,2,32,128]{4,3,2,1,0:T(8,128)(2,1)} %get-tuple-element.6.sums), custom_call_target="tpu_custom_call" | custom-call | tf_op jit(solution)/shard_map/pallas_call | solution.py:665
